TPU v7x, 32 devices: a whole 2x2x4 slice. The times are simulated.
32 devices in a mesh: groups: 2 (over y), ctx: 4 (over z), kvh: 2 (over x), sub: 2 (over core).
Axes of the slice: x: 2, y: 2, z: 4, core: 2. Of those that a mesh axis runs over, the one named last changes fastest.
Arguments:
- queries: bfloat16 [2048, 64, 128], P(('groups', 'ctx', 'sub'), 'kvh'), parts along dimension 0, may hold values from -8 to 8
- key_states: bfloat16 [1024, 8, 128], P(('groups', 'ctx'), 'kvh'), parts along dimension 0, may hold values from -8 to 8
- obs_positions: int32 [2048], P(('groups', 'ctx', 'sub')), parts along dimension 0, may hold values from 0 to 511, as said below
- block_lists: int32 [16, 8], P(('groups', 'ctx', 'sub')), parts along dimension 0, may hold values from -1 to 7, as said below
- bin_edges: int32 [258], P('groups'), parts along dimension 0, may hold values from 0 to 512, as said below
Outputs:
- key_mass: float32 [8, 1024], P('kvh', ('groups', 'ctx')), parts along dimension 1
- bin_density: float32 [8, 256], P('kvh', 'groups'), parts along dimension 1
There are 2 independent parts, one for each index of `groups`. A program takes and returns all parts, laid end to end along the dimension named above; each array names one. Nothing has to cross between parts.
Inputs may be any that keep to these rules, and one draw needn't show every extreme that they name: `obs_positions`: each aligned block of 128 entries holds distinct positions in increasing order. `block_lists`: each row names 1 to 8 distinct key blocks in its first entries and holds -1 in the others; some row names 8. `bin_edges`: strictly increasing from 0 to 512.
All inputs are finite; a program needn't handle non-finite values.
Results may differ from a plain program's by a relative error of at most 0.0003.
Values may be sent and summed in bfloat16 or wider, within the bound.
No kernel may reach another device: no remote copies, remote signals or barrier semaphores. Data moves between devices by JAX's collectives and lax.ppermute only.
A program may use at most 64 MiB of HBM per device.

v0:
```python
import math

import jax
import jax.numpy as jnp
from jax import lax
from jax.experimental import pallas as pl
from jax.experimental.pallas import tpu as pltpu
from jax.sharding import PartitionSpec as P


KB = 64
NEG = -1e30
LOG2E = math.log2(math.e)
VMEM = pl.BlockSpec(memory_space=pltpu.VMEM)


def xor_pairs(count, distance):
    return [(i, i ^ distance) for i in range(count)]


def visible_bias(positions, lists, owners, local_keys):
    rows = positions.shape[0]
    per_list = rows // lists.shape[0]
    key_pos = (owners[:, None] * local_keys + jnp.arange(local_keys, dtype=jnp.int32)).reshape(-1)
    key_block = key_pos // KB
    listed = jnp.any(lists[:, :, None] == key_block[None, None, :], axis=1)
    listed = jnp.broadcast_to(listed[:, None, :], (lists.shape[0], per_list, key_pos.shape[0]))
    listed = listed.reshape(rows, -1)
    own_block = key_block[None, :] == (positions // KB)[:, None]
    seen = (key_pos[None, :] <= positions[:, None]) & (listed | own_block)
    return jnp.where(seen, 0.0, NEG).astype(jnp.float32)


def mass_call(own_queries, sibling_queries, keys, order, bias, scale, factor):
    half, _, per_group, head_dim = own_queries.shape
    chunks = len(keys)
    groups, local_keys, _ = keys[0].shape
    total = chunks * local_keys
    step = max(8, min(half, (1 << 20) // (per_group * total)))

    def kernel(own_ref, sibling_ref, *refs):
        key_refs, bias_ref, out_ref, all_keys = refs[:chunks], refs[chunks], refs[-2], refs[-1]
        sub = lax.axis_index("sub")
        ctx = lax.axis_index("ctx")
        for index, key_ref in enumerate(key_refs):
            all_keys[:, index * local_keys : (index + 1) * local_keys, :] = key_ref[...]
        for group in range(groups):
            block_keys = all_keys[group]
            mass = jnp.zeros((per_group, total), jnp.float32)
            for part, query_ref in enumerate((own_ref, sibling_ref)):

                def advance(index, mass):
                    rows = query_ref[pl.ds(index * step, step), part * (sub * groups) + group]
                    scores = lax.dot_general(
                        rows.reshape(step * per_group, head_dim),
                        block_keys,
                        (((1,), (1,)), ((), ())),
                        preferred_element_type=jnp.float32,
                    ).reshape(step, per_group, total)
                    hidden = bias_ref[pl.ds(part * half + index * step, step), :]
                    scores = scores + hidden[:, None, :]
                    peak = jnp.max(scores, axis=-1, keepdims=True)
                    terms = jnp.exp2((scores - peak) * (scale * LOG2E))
                    weight = 1.0 / jnp.sum(terms, axis=-1, keepdims=True)
                    return mass + jnp.sum(terms * weight, axis=0)

                if step == half:
                    mass = advance(0, mass)
                else:
                    mass = lax.fori_loop(0, half // step, advance, mass)
            row = jnp.sum(mass, axis=0, keepdims=True) * factor
            for index in range(chunks):
                owner = jnp.bitwise_xor(ctx, (0, *order)[index])
                out_ref[pl.ds(group * chunks + owner, 1), :] = row[
                    :, index * local_keys : (index + 1) * local_keys
                ]

    return pl.pallas_call(
        kernel,
        out_shape=jax.ShapeDtypeStruct((groups * chunks, local_keys), jnp.float32),
        in_specs=[VMEM] * (3 + chunks),
        out_specs=VMEM,
        scratch_shapes=[pltpu.VMEM((groups, total, head_dim), jnp.bfloat16)],
        compiler_params=pltpu.CompilerParams(vmem_limit_bytes=32 << 20),
        cost_estimate=pl.CostEstimate(
            flops=4 * half * per_group * groups * total * head_dim,
            bytes_accessed=1 << 20,
            transcendentals=2 * half * per_group * groups * total,
        ),
    )(own_queries, sibling_queries, *keys, bias)


def finish_call(mine, theirs, edges, groups, chunks):
    rows, local_keys = mine.shape
    half = rows // 2
    bins = edges.shape[1]

    def kernel(mine_ref, theirs_ref, edges_ref, mass_ref, bins_ref, total):
        sub = lax.axis_index("sub")
        ctx = lax.axis_index("ctx")
        for part in range(2):
            place = jnp.bitwise_xor(sub, part) * half
            rows_here = slice(part * half, (part + 1) * half)
            total[pl.ds(place, half), :] = mine_ref[rows_here, :] + theirs_ref[rows_here, :]
        low, high = edges_ref[0:1, :], edges_ref[1:2, :]
        sums = jnp.zeros((2 * groups * 3, bins), jnp.float32)
        for chunk in range(chunks):
            values = jnp.concatenate(
                [total[group * chunks + chunk][None, :] for group in range(2 * groups)], axis=0
            )
            first = values.astype(jnp.bfloat16)
            rest = values - first.astype(jnp.float32)
            second = rest.astype(jnp.bfloat16)
            third = (rest - second.astype(jnp.float32)).astype(jnp.bfloat16)
            split = jnp.concatenate([first, second, third], axis=0)
            key_pos = chunk * local_keys + lax.broadcasted_iota(jnp.int32, (local_keys, bins), 0)
            member = jnp.where((key_pos >= low) & (key_pos < high), 1.0, 0.0).astype(jnp.bfloat16)
            sums = sums + jnp.dot(split, member, preferred_element_type=jnp.float32)
        count = 2 * groups
        summed = sums[:count] + sums[count : 2 * count] + sums[2 * count :]
        bins_ref[...] = summed / (high - low).astype(jnp.float32)
        for group in range(2 * groups):
            mass_ref[group : group + 1, :] = total[pl.ds(group * chunks + ctx, 1), :]

    return pl.pallas_call(
        kernel,
        out_shape=(
            jax.ShapeDtypeStruct((2 * groups, local_keys), jnp.float32),
            jax.ShapeDtypeStruct((2 * groups, bins), jnp.float32),
        ),
        in_specs=[VMEM] * 3,
        out_specs=(VMEM, VMEM),
        scratch_shapes=[pltpu.VMEM((rows, local_keys), jnp.float32)],
        compiler_params=pltpu.CompilerParams(vmem_limit_bytes=4 << 20),
    )(mine, theirs, edges)


def local(queries, key_states, obs_positions, block_lists, bin_edges):
    query_rows, heads_dev, head_dim = queries.shape
    local_keys, groups_dev, _ = key_states.shape
    per_group = heads_dev // groups_dev
    ctx_count = lax.axis_size("ctx")
    sub_count = lax.axis_size("sub")
    both_count = ctx_count * sub_count
    groups = groups_dev // sub_count
    sub = lax.axis_index("sub")
    ctx = lax.axis_index("ctx")
    scale = head_dim ** (-0.5)
    factor = ctx_count * local_keys / (query_rows * both_count * per_group)

    order = [2, 3, 1] if ctx_count == 4 else list(range(1, ctx_count))
    own_keys = lax.dynamic_slice_in_dim(key_states, sub * groups, groups, 1)
    own_keys = jnp.transpose(own_keys, (1, 0, 2))
    keys = [own_keys] + [
        lax.ppermute(own_keys, "ctx", xor_pairs(ctx_count, distance))
        for distance in order
    ]

    swap = xor_pairs(sub_count, 1)
    queries4 = queries.reshape(query_rows, groups_dev, per_group, head_dim)
    sibling_queries = lax.ppermute(queries4, "sub", swap)
    positions = jnp.concatenate([obs_positions, lax.ppermute(obs_positions, "sub", swap)])
    lists = jnp.concatenate([block_lists, lax.ppermute(block_lists, "sub", swap)])
    owners = jnp.bitwise_xor(ctx, jnp.array([0, *order], jnp.int32))
    bias = visible_bias(positions, lists, owners, local_keys)

    own_queries = lax.dynamic_slice_in_dim(queries4, sub * groups, groups, 1)
    mass = mass_call(own_queries, sibling_queries, keys, order, bias, scale, factor)

    near = lax.ppermute(mass, "ctx", xor_pairs(ctx_count, 1))
    aside = lax.ppermute(mass, "sub", swap)
    across = lax.ppermute(mass, ("ctx", "sub"), xor_pairs(both_count, 3))
    mine = jnp.concatenate([mass + near, aside + across])
    theirs = None
    distance = 2
    while distance < ctx_count:
        if theirs is not None:
            mine = mine + theirs
        theirs = lax.ppermute(mine, "ctx", xor_pairs(ctx_count, distance))
        distance *= 2
    edges = jnp.stack([bin_edges[:-1], bin_edges[1:]])
    return finish_call(mine, theirs, edges, groups, ctx_count)


def solution(mesh):
    return jax.shard_map(
        local,
        mesh=mesh,
        in_specs=(
            P(("groups", "ctx", "sub"), "kvh", None),
            P(("groups", "ctx"), "kvh", None),
            P(("groups", "ctx", "sub")),
            P(("groups", "ctx", "sub"), None),
            P("groups"),
        ),
        out_specs=(P("kvh", ("groups", "ctx")), P("kvh", "groups")),
        check_vma=False,
    )
```

profile of v0, /device:TPU:0, one launch (start us, length us, event | category | flops | bytes accessed | tf_op | source)
XLA Modules:
  0.0 25.7 jit_solution(16761212103798424893)
XLA Ops:
  0.7 0.9 %copy-done = bf16[128,4,128]{2,1,0:T(4,128)(2,1)S(1)} copy-done((bf16[128,4,128]{2,1,0:T(4,128)(2,1)S(1)}, bf16[128,4,128]{2,1,0:T(4,128)(2,1)}, u32[]{:S(2)}) %copy-start) | copy-done | bytes 131096
  1.5 0.1 constant_dynamic-slice_fusion
  1.6 4.1 %collective-permute-start.1 = (bf16[2,128,128]{2,1,0:T(8,128)(2,1)S(1)}, bf16[2,128,128]{2,1,0:T(8,128)(2,1)S(1)}, u32[]{:S(2)}, u32[]{:S(2)}) collective-permute-start(bf16[2,128,128]{2,1,0:T(8,128)(2,1)S(1)} %bitcast.34), channel_id=1, source_target_pairs={{0,8},{4,12},{8,0},{12,4},{1,9},{5,13},{9,1},{13,5},{2,10},{6,14},... | collective-permute-start | bytes 196616 | tf_op jit(solution)/shard_map/ppermute | solution.py:155
  5.8 1.3 %collective-permute-start.2 = (bf16[2,128,128]{2,1,0:T(8,128)(2,1)S(1)}, bf16[2,128,128]{2,1,0:T(8,128)(2,1)S(1)}, u32[]{:S(2)}, u32[]{:S(2)}) collective-permute-start(bf16[2,128,128]{2,1,0:T(8,128)(2,1)S(1)} %bitcast.35), channel_id=1, source_target_pairs={{0,12},{4,8},{8,4},{12,0},{1,13},{5,9},{9,5},{13,1},{2,14},{6,10},... | collective-permute-start | bytes 196616 | tf_op jit(solution)/shard_map/ppermute | solution.py:155
  7.1 0.2 collective-permute-start.3
  7.4 0.5 %collective-permute-start.5 = (s32[1,8]{1,0:T(1,128)S(1)}, s32[1,8]{1,0:T(1,128)S(1)}, u32[]{:S(2)}, u32[]{:S(2)}) collective-permute-start(s32[1,8]{1,0:T(1,128)S(1)} %copy-done.2), channel_id=1, source_target_pairs={{0,1},{1,0},{2,3},{3,2},{4,5},{5,4},{6,7},{7,6},{8,9},{9,8},{10,11... | collective-permute-start | bytes 104 | tf_op jit(solution)/shard_map/ppermute | solution.py:163
  7.9 1.1 %constant_dynamic-slice_fusion.1.own_ref = bf16[128,2,8,128]{3,2,1,0:T(8,128)(2,1)S(1)} fusion(bf16[128,4,8,128]{3,2,1,0:T(8,128)(2,1)} %bitcast.39, s32[]{:T(128)S(6)} %select_n.30), kind=kLoop, calls=%fused_computation.27 | loop fusion | bytes 1048580 | tf_op jit(solution)/shard_map/dynamic_slice | solution.py:167
  9.0 0.6 %copy-done.4 = s32[4]{0:T(128)S(1)} copy-done((s32[4]{0:T(128)S(1)}, s32[4]{0:T(128)}, u32[]{:S(2)}) %copy-start.4) | copy-done | bytes 40
  9.6 0.6 %copy-done.3 = s32[128]{0:T(128)S(1)} copy-done((s32[128]{0:T(128)S(1)}, s32[128]{0:T(128)}, u32[]{:S(2)}) %copy-start.3) | copy-done | bytes 536
  10.3 0.1 add_select_fusion
  10.4 0.1 add_bitcast_fusion
  10.5 0.1 compare_reduce_fusion
  10.6 1.0 %collective-permute-done.4 = s32[128]{0:T(128)S(1)} collective-permute-done((s32[128]{0:T(128)S(1)}, s32[128]{0:T(128)S(1)}, u32[]{:S(2)}, u32[]{:S(2)}) %collective-permute-start.4) | collective-permute-done | bytes 544 | tf_op jit(solution)/shard_map/ppermute | solution.py:162
  11.6 0.2 fusion.1.refs_4_
  11.9 0.1 collective-permute-done.3.refs_3_
  12.1 2.8 %shard_map.77 = f32[8,128]{1,0:T(8,128)S(1)} custom-call(bf16[128,2,8,128]{3,2,1,0:T(8,128)(2,1)S(1)} %constant_dynamic-slice_fusion.1.own_ref, bf16[128,4,8,128]{3,2,1,0:T(8,128)(2,1)S(1)} %collective-permute-done.sibling_ref, bf16[2,128,128]{2,1,0:T(8,128)(2,1)S(1)} %bitcast.37, bf16[2,128,128]{2,1,0:T(8,128)(2,1)S(1)} %collective-permute-done.1.refs_1_, ...), custom_call_target="tpu_custom_call" | custom-call | flops 536870912 | bytes 1048576 | tf_op jit(solution)/shard_map/pallas_call | solution.py:78
  14.9 0.1 collective-permute-start.7
  15.0 1.7 %collective-permute-start.8 = (f32[8,128]{1,0:T(8,128)S(1)}, f32[8,128]{1,0:T(8,128)S(1)}, u32[]{:S(2)}, u32[]{:S(2)}) collective-permute-start(f32[8,128]{1,0:T(8,128)S(1)} %shard_map.77), channel_id=1, source_target_pairs={{0,5},{1,4},{4,1},{5,0},{8,13},{9,12},{12,9},{13,8},{2,7},{3,6},{6... | collective-permute-start | bytes 12296 | tf_op jit(solution)/shard_map/ppermute | solution.py:172
  16.7 0.4 %collective-permute-start.6 = (f32[8,128]{1,0:T(8,128)S(1)}, f32[8,128]{1,0:T(8,128)S(1)}, u32[]{:S(2)}, u32[]{:S(2)}) collective-permute-start(f32[8,128]{1,0:T(8,128)S(1)} %shard_map.77), channel_id=1, source_target_pairs={{0,4},{4,0},{8,12},{12,8},{1,5},{5,1},{9,13},{13,9},{2,6},{6,2},{1... | collective-permute-start | bytes 12296 | tf_op jit(solution)/shard_map/ppermute | solution.py:170
  17.1 0.1 slice_bitcast_fusion.1
  17.2 3.1 %collective-permute-done.6 = f32[8,128]{1,0:T(8,128)S(1)} collective-permute-done((f32[8,128]{1,0:T(8,128)S(1)}, f32[8,128]{1,0:T(8,128)S(1)}, u32[]{:S(2)}, u32[]{:S(2)}) %collective-permute-start.6) | collective-permute-done | bytes 4128 | tf_op jit(solution)/shard_map/ppermute | solution.py:170
  20.3 2.0 %collective-permute-start.9 = (f32[16,128]{1,0:T(8,128)S(1)}, f32[16,128]{1,0:T(8,128)S(1)}, u32[]{:S(2)}, u32[]{:S(2)}) collective-permute-start(f32[16,128]{1,0:T(8,128)S(1)} %pad_maximum_fusion.mine_ref), channel_id=1, source_target_pairs={{0,8},{4,12},{8,0},{12,4},{1,9},{5,13},{9,1},{13,5},{2,10},{6,14},... | collective-permute-start | bytes 24584 | tf_op jit(solution)/shard_map/ppermute | solution.py:179
  22.3 2.6 %collective-permute-done.9.theirs_ref = f32[16,128]{1,0:T(8,128)S(1)} collective-permute-done((f32[16,128]{1,0:T(8,128)S(1)}, f32[16,128]{1,0:T(8,128)S(1)}, u32[]{:S(2)}, u32[]{:S(2)}) %collective-permute-start.9) | collective-permute-done | bytes 8224 | tf_op jit(solution)/shard_map/ppermute | solution.py:179
  24.9 0.8 %shard_map.78 = (f32[4,128]{1,0:T(4,128)}, f32[4,128]{1,0:T(4,128)}) custom-call(f32[16,128]{1,0:T(8,128)S(1)} %pad_maximum_fusion.mine_ref, f32[16,128]{1,0:T(8,128)S(1)} %collective-permute-done.9.theirs_ref, s32[2,128]{1,0:T(2,128)S(1)} %pad_add_fusion.1.edges_ref), custom_call_target="tpu_custom_call" | custom-call | tf_op jit(solution)/shard_map/pallas_call | solution.py:125
  (26 shorter events, 0.2 us)
Async XLA Ops:
  0.6 0.9 %copy-start = (bf16[128,4,128]{2,1,0:T(4,128)(2,1)S(1)}, bf16[128,4,128]{2,1,0:T(4,128)(2,1)}, u32[]{:S(2)}) copy-start(bf16[128,4,128]{2,1,0:T(4,128)(2,1)} %param.7) | copy-start | bytes 393220
  1.6 5.7 %copy-start.2 = (s32[1,8]{1,0:T(1,128)S(1)}, s32[1,8]{1,0:T(1,128)}, u32[]{:S(2)}) copy-start(s32[1,8]{1,0:T(1,128)} %param.9) | copy-start | bytes 100
  1.6 10.2 %collective-permute-start.1 = (bf16[2,128,128]{2,1,0:T(8,128)(2,1)S(1)}, bf16[2,128,128]{2,1,0:T(8,128)(2,1)S(1)}, u32[]{:S(2)}, u32[]{:S(2)}) collective-permute-start(bf16[2,128,128]{2,1,0:T(8,128)(2,1)S(1)} %bitcast.34), channel_id=1, source_target_pairs={{0,8},{4,12},{8,0},{12,4},{1,9},{5,13},{9,1},{13,5},{2,10},{6,14},... | collective-permute-start | bytes 196616 | tf_op jit(solution)/shard_map/ppermute | solution.py:155
  5.8 6.2 %collective-permute-start.2 = (bf16[2,128,128]{2,1,0:T(8,128)(2,1)S(1)}, bf16[2,128,128]{2,1,0:T(8,128)(2,1)S(1)}, u32[]{:S(2)}, u32[]{:S(2)}) collective-permute-start(bf16[2,128,128]{2,1,0:T(8,128)(2,1)S(1)} %bitcast.35), channel_id=1, source_target_pairs={{0,12},{4,8},{8,4},{12,0},{1,13},{5,9},{9,5},{13,1},{2,14},{6,10},... | collective-permute-start | bytes 196616 | tf_op jit(solution)/shard_map/ppermute | solution.py:155
  7.1 5.0 %collective-permute-start.3 = (bf16[2,128,128]{2,1,0:T(8,128)(2,1)S(1)}, bf16[2,128,128]{2,1,0:T(8,128)(2,1)S(1)}, u32[]{:S(2)}, u32[]{:S(2)}) collective-permute-start(bf16[2,128,128]{2,1,0:T(8,128)(2,1)S(1)} %bitcast.36), channel_id=1, source_target_pairs={{0,4},{4,0},{8,12},{12,8},{1,5},{5,1},{9,13},{13,9},{2,6},{6,2},{1... | collective-permute-start | bytes 196616 | tf_op jit(solution)/shard_map/ppermute | solution.py:155
  7.4 4.7 %collective-permute-start = (bf16[128,4,8,128]{3,2,1,0:T(8,128)(2,1)}, bf16[128,4,8,128]{3,2,1,0:T(8,128)(2,1)S(1)}, u32[]{:S(2)}, u32[]{:S(2)}) collective-permute-start(bf16[128,4,8,128]{3,2,1,0:T(8,128)(2,1)} %bitcast.38), channel_id=1, source_target_pairs={{0,1},{1,0},{2,3},{3,2},{4,5},{5,4},{6,7},{7,6},{8,9},{9,8},{10,11... | collective-permute-start | bytes 3145736 | tf_op jit(solution)/shard_map/ppermute | solution.py:161
  7.4 3.1 %collective-permute-start.5 = (s32[1,8]{1,0:T(1,128)S(1)}, s32[1,8]{1,0:T(1,128)S(1)}, u32[]{:S(2)}, u32[]{:S(2)}) collective-permute-start(s32[1,8]{1,0:T(1,128)S(1)} %copy-done.2), channel_id=1, source_target_pairs={{0,1},{1,0},{2,3},{3,2},{4,5},{5,4},{6,7},{7,6},{8,9},{9,8},{10,11... | collective-permute-start | bytes 104 | tf_op jit(solution)/shard_map/ppermute | solution.py:163
  9.0 0.7 %copy-start.4 = (s32[4]{0:T(128)S(1)}, s32[4]{0:T(128)}, u32[]{:S(2)}) copy-start(s32[4]{0:T(128)} %constant.49.clone) | copy-start | bytes 52
  9.6 0.7 %copy-start.3 = (s32[128]{0:T(128)S(1)}, s32[128]{0:T(128)}, u32[]{:S(2)}) copy-start(s32[128]{0:T(128)} %param.8) | copy-start | bytes 1540
  10.4 1.2 %collective-permute-start.4 = (s32[128]{0:T(128)S(1)}, s32[128]{0:T(128)S(1)}, u32[]{:S(2)}, u32[]{:S(2)}) collective-permute-start(s32[128]{0:T(128)S(1)} %copy-done.3), channel_id=1, source_target_pairs={{0,1},{1,0},{2,3},{3,2},{4,5},{5,4},{6,7},{7,6},{8,9},{9,8},{10,11... | collective-permute-start | bytes 1544 | tf_op jit(solution)/shard_map/ppermute | solution.py:162
  11.9 5.2 %copy-start.1 = (s32[129]{0:T(256)S(1)}, s32[129]{0:T(256)}, u32[]{:S(2)}) copy-start(s32[129]{0:T(256)} %param.10) | copy-start | bytes 1552
  14.9 5.4 %collective-permute-start.7 = (f32[8,128]{1,0:T(8,128)S(1)}, f32[8,128]{1,0:T(8,128)S(1)}, u32[]{:S(2)}, u32[]{:S(2)}) collective-permute-start(f32[8,128]{1,0:T(8,128)S(1)} %shard_map.77), channel_id=1, source_target_pairs={{0,1},{1,0},{2,3},{3,2},{4,5},{5,4},{6,7},{7,6},{8,9},{9,8},{10,11... | collective-permute-start | bytes 12296 | tf_op jit(solution)/shard_map/ppermute | solution.py:171
  15.0 5.3 %collective-permute-start.8 = (f32[8,128]{1,0:T(8,128)S(1)}, f32[8,128]{1,0:T(8,128)S(1)}, u32[]{:S(2)}, u32[]{:S(2)}) collective-permute-start(f32[8,128]{1,0:T(8,128)S(1)} %shard_map.77), channel_id=1, source_target_pairs={{0,5},{1,4},{4,1},{5,0},{8,13},{9,12},{12,9},{13,8},{2,7},{3,6},{6... | collective-permute-start | bytes 12296 | tf_op jit(solution)/shard_map/ppermute | solution.py:172
  16.7 3.6 %collective-permute-start.6 = (f32[8,128]{1,0:T(8,128)S(1)}, f32[8,128]{1,0:T(8,128)S(1)}, u32[]{:S(2)}, u32[]{:S(2)}) collective-permute-start(f32[8,128]{1,0:T(8,128)S(1)} %shard_map.77), channel_id=1, source_target_pairs={{0,4},{4,0},{8,12},{12,8},{1,5},{5,1},{9,13},{13,9},{2,6},{6,2},{1... | collective-permute-start | bytes 12296 | tf_op jit(solution)/shard_map/ppermute | solution.py:170
  20.3 4.6 %collective-permute-start.9 = (f32[16,128]{1,0:T(8,128)S(1)}, f32[16,128]{1,0:T(8,128)S(1)}, u32[]{:S(2)}, u32[]{:S(2)}) collective-permute-start(f32[16,128]{1,0:T(8,128)S(1)} %pad_maximum_fusion.mine_ref), channel_id=1, source_target_pairs={{0,8},{4,12},{8,0},{12,4},{1,9},{5,13},{9,1},{13,5},{2,10},{6,14},... | collective-permute-start | bytes 24584 | tf_op jit(solution)/shard_map/ppermute | solution.py:179
where the time goes:
time: 25.9 us; the launch traced here: 25.7 us
  starting transfers between devices  10.4 us (40%)
  waiting for transfers between devices  6.98 us (27%)
  Pallas kernels  3.53 us (14%)
  local copies, waits for them, and re-layouts  3.47 us (13%)
  between operations  0.76 us (3%)
  other arithmetic  0.49 us (2%)
    ppermute x3, starting transfers between devices, local(): lax.ppermute(own_keys, 'ctx', xor_pairs(ctx_count, distance))  5.71 us
    ppermute x1, waiting for transfers between devices, local(): near = lax.ppermute(mass, 'ctx', xor_pairs(ctx_count, 1))  3.12 us
    pallas_call x1, Pallas kernels, mass_call(): pl.pallas_call(kernel, out_shape=jax.ShapeDtypeStruct((groups * chunks, l...  2.78 us
    ppermute x1, waiting for transfers between devices, local(): theirs = lax.ppermute(mine, 'ctx', xor_pairs(ctx_count, distance))  2.59 us
    unnamed x12, local copies, waits for them, and re-layouts  2.24 us
    ppermute x1, starting transfers between devices, local(): theirs = lax.ppermute(mine, 'ctx', xor_pairs(ctx_count, distance))  2.01 us
    ppermute x1, starting transfers between devices, local(): across = lax.ppermute(mass, ('ctx', 'sub'), xor_pairs(both_count, 3))  1.71 us
    dynamic_slice x1, local copies, waits for them, and re-layouts, local(): own_queries = lax.dynamic_slice_in_dim(queries4, sub * groups, groups, 1)  1.08 us
  transfers between devices with their start and end apart: 10, of which 5 were waited for; matrix products, arithmetic and copies ran while one was open for 6% of the time, Pallas kernels for 0%

commit v1 on v0

--- a/solution.py
+++ b/solution.py
@@ -57,8 +57,16 @@
                         (((1,), (1,)), ((), ())),
                         preferred_element_type=jnp.float32,
                     ).reshape(step, per_group, total)
-                    hidden = bias_ref[pl.ds(part * half + index * step, step), :]
-                    scores = scores + hidden[:, None, :]
+                    first = part * half + index * step
+                    if isinstance(first, int):
+                        spread = [
+                            bias_ref[pl.ds(first + row, per_group, stride=0), :]
+                            for row in range(step)
+                        ]
+                        hidden = jnp.stack(spread)
+                    else:
+                        hidden = bias_ref[pl.ds(first, step), :][:, None, :]
+                    scores = scores + hidden
                     peak = jnp.max(scores, axis=-1, keepdims=True)
                     terms = jnp.exp2((scores - peak) * (scale * LOG2E))
                     weight = 1.0 / jnp.sum(terms, axis=-1, keepdims=True)

time: 25.9 us -> 25.6 us (0.988)
  transfers between devices with their start and end apart: 10 -> 10, of which waited for: 5 -> 5; matrix products, arithmetic and copies ran while one was open for 6% -> 7% of each run, Pallas kernels for 0% -> 0%
where the time goes in v1:
time: 25.6 us; the launch traced here: 25.4 us
  starting transfers between devices  10.4 us (41%)
  waiting for transfers between devices  6.98 us (27%)
  local copies, waits for them, and re-layouts  3.47 us (14%)
  Pallas kernels  3.28 us (13%)
  between operations  0.76 us (3%)
  other arithmetic  0.49 us (2%)
    ppermute x3, starting transfers between devices, local(): lax.ppermute(own_keys, 'ctx', xor_pairs(ctx_count, distance))  5.71 us
    ppermute x1, waiting for transfers between devices, local(): near = lax.ppermute(mass, 'ctx', xor_pairs(ctx_count, 1))  3.12 us
    ppermute x1, waiting for transfers between devices, local(): theirs = lax.ppermute(mine, 'ctx', xor_pairs(ctx_count, distance))  2.59 us
    pallas_call x1, Pallas kernels, mass_call(): pl.pallas_call(kernel, out_shape=jax.ShapeDtypeStruct((groups * chunks, l...  2.52 us
    unnamed x12, local copies, waits for them, and re-layouts  2.24 us
    ppermute x1, starting transfers between devices, local(): theirs = lax.ppermute(mine, 'ctx', xor_pairs(ctx_count, distance))  2.01 us
    ppermute x1, starting transfers between devices, local(): across = lax.ppermute(mass, ('ctx', 'sub'), xor_pairs(both_count, 3))  1.71 us
    dynamic_slice x1, local copies, waits for them, and re-layouts, local(): own_queries = lax.dynamic_slice_in_dim(queries4, sub * groups, groups, 1)  1.08 us
  transfers between devices with their start and end apart: 10, of which 5 were waited for; matrix products, arithmetic and copies ran while one was open for 7% of the time, Pallas kernels for 0%

profile of v1, /device:TPU:0, one launch (start us, length us, event | category | flops | bytes accessed | tf_op | source)
XLA Modules:
  0.0 25.4 jit_solution(14107129224745756030)
XLA Ops:
  0.7 0.9 %copy-done = bf16[128,4,128]{2,1,0:T(4,128)(2,1)S(1)} copy-done((bf16[128,4,128]{2,1,0:T(4,128)(2,1)S(1)}, bf16[128,4,128]{2,1,0:T(4,128)(2,1)}, u32[]{:S(2)}) %copy-start) | copy-done | bytes 131096
  1.5 0.1 constant_dynamic-slice_fusion
  1.6 4.1 %collective-permute-start.1 = (bf16[2,128,128]{2,1,0:T(8,128)(2,1)S(1)}, bf16[2,128,128]{2,1,0:T(8,128)(2,1)S(1)}, u32[]{:S(2)}, u32[]{:S(2)}) collective-permute-start(bf16[2,128,128]{2,1,0:T(8,128)(2,1)S(1)} %bitcast.34), channel_id=1, source_target_pairs={{0,8},{4,12},{8,0},{12,4},{1,9},{5,13},{9,1},{13,5},{2,10},{6,14},... | collective-permute-start | bytes 196616 | tf_op jit(solution)/shard_map/ppermute | solution.py:163
  5.8 1.3 %collective-permute-start.2 = (bf16[2,128,128]{2,1,0:T(8,128)(2,1)S(1)}, bf16[2,128,128]{2,1,0:T(8,128)(2,1)S(1)}, u32[]{:S(2)}, u32[]{:S(2)}) collective-permute-start(bf16[2,128,128]{2,1,0:T(8,128)(2,1)S(1)} %bitcast.35), channel_id=1, source_target_pairs={{0,12},{4,8},{8,4},{12,0},{1,13},{5,9},{9,5},{13,1},{2,14},{6,10},... | collective-permute-start | bytes 196616 | tf_op jit(solution)/shard_map/ppermute | solution.py:163
  7.1 0.2 collective-permute-start.3
  7.4 0.5 %collective-permute-start.5 = (s32[1,8]{1,0:T(1,128)S(1)}, s32[1,8]{1,0:T(1,128)S(1)}, u32[]{:S(2)}, u32[]{:S(2)}) collective-permute-start(s32[1,8]{1,0:T(1,128)S(1)} %copy-done.2), channel_id=1, source_target_pairs={{0,1},{1,0},{2,3},{3,2},{4,5},{5,4},{6,7},{7,6},{8,9},{9,8},{10,11... | collective-permute-start | bytes 104 | tf_op jit(solution)/shard_map/ppermute | solution.py:171
  7.9 1.1 %constant_dynamic-slice_fusion.1.own_ref = bf16[128,2,8,128]{3,2,1,0:T(8,128)(2,1)S(1)} fusion(bf16[128,4,8,128]{3,2,1,0:T(8,128)(2,1)} %bitcast.39, s32[]{:T(128)S(6)} %select_n.30), kind=kLoop, calls=%fused_computation.27 | loop fusion | bytes 1048580 | tf_op jit(solution)/shard_map/dynamic_slice | solution.py:175
  9.0 0.6 %copy-done.4 = s32[4]{0:T(128)S(1)} copy-done((s32[4]{0:T(128)S(1)}, s32[4]{0:T(128)}, u32[]{:S(2)}) %copy-start.4) | copy-done | bytes 40
  9.6 0.6 %copy-done.3 = s32[128]{0:T(128)S(1)} copy-done((s32[128]{0:T(128)S(1)}, s32[128]{0:T(128)}, u32[]{:S(2)}) %copy-start.3) | copy-done | bytes 536
  10.3 0.1 add_select_fusion
  10.4 0.1 add_bitcast_fusion
  10.5 0.1 compare_reduce_fusion
  10.6 1.0 %collective-permute-done.4 = s32[128]{0:T(128)S(1)} collective-permute-done((s32[128]{0:T(128)S(1)}, s32[128]{0:T(128)S(1)}, u32[]{:S(2)}, u32[]{:S(2)}) %collective-permute-start.4) | collective-permute-done | bytes 544 | tf_op jit(solution)/shard_map/ppermute | solution.py:170
  11.6 0.2 fusion.1.refs_4_
  11.9 0.1 collective-permute-done.3.refs_3_
  12.1 2.5 %shard_map.77 = f32[8,128]{1,0:T(8,128)S(1)} custom-call(bf16[128,2,8,128]{3,2,1,0:T(8,128)(2,1)S(1)} %constant_dynamic-slice_fusion.1.own_ref, bf16[128,4,8,128]{3,2,1,0:T(8,128)(2,1)S(1)} %collective-permute-done.sibling_ref, bf16[2,128,128]{2,1,0:T(8,128)(2,1)S(1)} %bitcast.37, bf16[2,128,128]{2,1,0:T(8,128)(2,1)S(1)} %collective-permute-done.1.refs_1_, ...), custom_call_target="tpu_custom_call" | custom-call | flops 536870912 | bytes 1048576 | tf_op jit(solution)/shard_map/pallas_call | solution.py:86
  14.6 0.1 collective-permute-start.7
  14.7 1.7 %collective-permute-start.8 = (f32[8,128]{1,0:T(8,128)S(1)}, f32[8,128]{1,0:T(8,128)S(1)}, u32[]{:S(2)}, u32[]{:S(2)}) collective-permute-start(f32[8,128]{1,0:T(8,128)S(1)} %shard_map.77), channel_id=1, source_target_pairs={{0,5},{1,4},{4,1},{5,0},{8,13},{9,12},{12,9},{13,8},{2,7},{3,6},{6... | collective-permute-start | bytes 12296 | tf_op jit(solution)/shard_map/ppermute | solution.py:180
  16.4 0.4 %collective-permute-start.6 = (f32[8,128]{1,0:T(8,128)S(1)}, f32[8,128]{1,0:T(8,128)S(1)}, u32[]{:S(2)}, u32[]{:S(2)}) collective-permute-start(f32[8,128]{1,0:T(8,128)S(1)} %shard_map.77), channel_id=1, source_target_pairs={{0,4},{4,0},{8,12},{12,8},{1,5},{5,1},{9,13},{13,9},{2,6},{6,2},{1... | collective-permute-start | bytes 12296 | tf_op jit(solution)/shard_map/ppermute | solution.py:178
  16.8 0.1 slice_bitcast_fusion.1
  16.9 3.1 %collective-permute-done.6 = f32[8,128]{1,0:T(8,128)S(1)} collective-permute-done((f32[8,128]{1,0:T(8,128)S(1)}, f32[8,128]{1,0:T(8,128)S(1)}, u32[]{:S(2)}, u32[]{:S(2)}) %collective-permute-start.6) | collective-permute-done | bytes 4128 | tf_op jit(solution)/shard_map/ppermute | solution.py:178
  20.1 2.0 %collective-permute-start.9 = (f32[16,128]{1,0:T(8,128)S(1)}, f32[16,128]{1,0:T(8,128)S(1)}, u32[]{:S(2)}, u32[]{:S(2)}) collective-permute-start(f32[16,128]{1,0:T(8,128)S(1)} %pad_maximum_fusion.mine_ref), channel_id=1, source_target_pairs={{0,8},{4,12},{8,0},{12,4},{1,9},{5,13},{9,1},{13,5},{2,10},{6,14},... | collective-permute-start | bytes 24584 | tf_op jit(solution)/shard_map/ppermute | solution.py:187
  22.1 2.6 %collective-permute-done.9.theirs_ref = f32[16,128]{1,0:T(8,128)S(1)} collective-permute-done((f32[16,128]{1,0:T(8,128)S(1)}, f32[16,128]{1,0:T(8,128)S(1)}, u32[]{:S(2)}, u32[]{:S(2)}) %collective-permute-start.9) | collective-permute-done | bytes 8224 | tf_op jit(solution)/shard_map/ppermute | solution.py:187
  24.7 0.8 %shard_map.78 = (f32[4,128]{1,0:T(4,128)}, f32[4,128]{1,0:T(4,128)}) custom-call(f32[16,128]{1,0:T(8,128)S(1)} %pad_maximum_fusion.mine_ref, f32[16,128]{1,0:T(8,128)S(1)} %collective-permute-done.9.theirs_ref, s32[2,128]{1,0:T(2,128)S(1)} %pad_add_fusion.1.edges_ref), custom_call_target="tpu_custom_call" | custom-call | tf_op jit(solution)/shard_map/pallas_call | solution.py:133
  (26 shorter events, 0.2 us)
Async XLA Ops:
  0.6 0.9 %copy-start = (bf16[128,4,128]{2,1,0:T(4,128)(2,1)S(1)}, bf16[128,4,128]{2,1,0:T(4,128)(2,1)}, u32[]{:S(2)}) copy-start(bf16[128,4,128]{2,1,0:T(4,128)(2,1)} %param.7) | copy-start | bytes 393220
  1.6 5.7 %copy-start.2 = (s32[1,8]{1,0:T(1,128)S(1)}, s32[1,8]{1,0:T(1,128)}, u32[]{:S(2)}) copy-start(s32[1,8]{1,0:T(1,128)} %param.9) | copy-start | bytes 100
  1.6 10.2 %collective-permute-start.1 = (bf16[2,128,128]{2,1,0:T(8,128)(2,1)S(1)}, bf16[2,128,128]{2,1,0:T(8,128)(2,1)S(1)}, u32[]{:S(2)}, u32[]{:S(2)}) collective-permute-start(bf16[2,128,128]{2,1,0:T(8,128)(2,1)S(1)} %bitcast.34), channel_id=1, source_target_pairs={{0,8},{4,12},{8,0},{12,4},{1,9},{5,13},{9,1},{13,5},{2,10},{6,14},... | collective-permute-start | bytes 196616 | tf_op jit(solution)/shard_map/ppermute | solution.py:163
  5.8 6.2 %collective-permute-start.2 = (bf16[2,128,128]{2,1,0:T(8,128)(2,1)S(1)}, bf16[2,128,128]{2,1,0:T(8,128)(2,1)S(1)}, u32[]{:S(2)}, u32[]{:S(2)}) collective-permute-start(bf16[2,128,128]{2,1,0:T(8,128)(2,1)S(1)} %bitcast.35), channel_id=1, source_target_pairs={{0,12},{4,8},{8,4},{12,0},{1,13},{5,9},{9,5},{13,1},{2,14},{6,10},... | collective-permute-start | bytes 196616 | tf_op jit(solution)/shard_map/ppermute | solution.py:163
  7.1 5.0 %collective-permute-start.3 = (bf16[2,128,128]{2,1,0:T(8,128)(2,1)S(1)}, bf16[2,128,128]{2,1,0:T(8,128)(2,1)S(1)}, u32[]{:S(2)}, u32[]{:S(2)}) collective-permute-start(bf16[2,128,128]{2,1,0:T(8,128)(2,1)S(1)} %bitcast.36), channel_id=1, source_target_pairs={{0,4},{4,0},{8,12},{12,8},{1,5},{5,1},{9,13},{13,9},{2,6},{6,2},{1... | collective-permute-start | bytes 196616 | tf_op jit(solution)/shard_map/ppermute | solution.py:163
  7.4 4.7 %collective-permute-start = (bf16[128,4,8,128]{3,2,1,0:T(8,128)(2,1)}, bf16[128,4,8,128]{3,2,1,0:T(8,128)(2,1)S(1)}, u32[]{:S(2)}, u32[]{:S(2)}) collective-permute-start(bf16[128,4,8,128]{3,2,1,0:T(8,128)(2,1)} %bitcast.38), channel_id=1, source_target_pairs={{0,1},{1,0},{2,3},{3,2},{4,5},{5,4},{6,7},{7,6},{8,9},{9,8},{10,11... | collective-permute-start | bytes 3145736 | tf_op jit(solution)/shard_map/ppermute | solution.py:169
  7.4 3.1 %collective-permute-start.5 = (s32[1,8]{1,0:T(1,128)S(1)}, s32[1,8]{1,0:T(1,128)S(1)}, u32[]{:S(2)}, u32[]{:S(2)}) collective-permute-start(s32[1,8]{1,0:T(1,128)S(1)} %copy-done.2), channel_id=1, source_target_pairs={{0,1},{1,0},{2,3},{3,2},{4,5},{5,4},{6,7},{7,6},{8,9},{9,8},{10,11... | collective-permute-start | bytes 104 | tf_op jit(solution)/shard_map/ppermute | solution.py:171
  9.0 0.7 %copy-start.4 = (s32[4]{0:T(128)S(1)}, s32[4]{0:T(128)}, u32[]{:S(2)}) copy-start(s32[4]{0:T(128)} %constant.49.clone) | copy-start | bytes 52
  9.6 0.7 %copy-start.3 = (s32[128]{0:T(128)S(1)}, s32[128]{0:T(128)}, u32[]{:S(2)}) copy-start(s32[128]{0:T(128)} %param.8) | copy-start | bytes 1540
  10.4 1.2 %collective-permute-start.4 = (s32[128]{0:T(128)S(1)}, s32[128]{0:T(128)S(1)}, u32[]{:S(2)}, u32[]{:S(2)}) collective-permute-start(s32[128]{0:T(128)S(1)} %copy-done.3), channel_id=1, source_target_pairs={{0,1},{1,0},{2,3},{3,2},{4,5},{5,4},{6,7},{7,6},{8,9},{9,8},{10,11... | collective-permute-start | bytes 1544 | tf_op jit(solution)/shard_map/ppermute | solution.py:170
  11.9 5.0 %copy-start.1 = (s32[129]{0:T(256)S(1)}, s32[129]{0:T(256)}, u32[]{:S(2)}) copy-start(s32[129]{0:T(256)} %param.10) | copy-start | bytes 1552
  14.6 5.4 %collective-permute-start.7 = (f32[8,128]{1,0:T(8,128)S(1)}, f32[8,128]{1,0:T(8,128)S(1)}, u32[]{:S(2)}, u32[]{:S(2)}) collective-permute-start(f32[8,128]{1,0:T(8,128)S(1)} %shard_map.77), channel_id=1, source_target_pairs={{0,1},{1,0},{2,3},{3,2},{4,5},{5,4},{6,7},{7,6},{8,9},{9,8},{10,11... | collective-permute-start | bytes 12296 | tf_op jit(solution)/shard_map/ppermute | solution.py:179
  14.7 5.3 %collective-permute-start.8 = (f32[8,128]{1,0:T(8,128)S(1)}, f32[8,128]{1,0:T(8,128)S(1)}, u32[]{:S(2)}, u32[]{:S(2)}) collective-permute-start(f32[8,128]{1,0:T(8,128)S(1)} %shard_map.77), channel_id=1, source_target_pairs={{0,5},{1,4},{4,1},{5,0},{8,13},{9,12},{12,9},{13,8},{2,7},{3,6},{6... | collective-permute-start | bytes 12296 | tf_op jit(solution)/shard_map/ppermute | solution.py:180
  16.4 3.6 %collective-permute-start.6 = (f32[8,128]{1,0:T(8,128)S(1)}, f32[8,128]{1,0:T(8,128)S(1)}, u32[]{:S(2)}, u32[]{:S(2)}) collective-permute-start(f32[8,128]{1,0:T(8,128)S(1)} %shard_map.77), channel_id=1, source_target_pairs={{0,4},{4,0},{8,12},{12,8},{1,5},{5,1},{9,13},{13,9},{2,6},{6,2},{1... | collective-permute-start | bytes 12296 | tf_op jit(solution)/shard_map/ppermute | solution.py:178
  20.1 4.6 %collective-permute-start.9 = (f32[16,128]{1,0:T(8,128)S(1)}, f32[16,128]{1,0:T(8,128)S(1)}, u32[]{:S(2)}, u32[]{:S(2)}) collective-permute-start(f32[16,128]{1,0:T(8,128)S(1)} %pad_maximum_fusion.mine_ref), channel_id=1, source_target_pairs={{0,8},{4,12},{8,0},{12,4},{1,9},{5,13},{9,1},{13,5},{2,10},{6,14},... | collective-permute-start | bytes 24584 | tf_op jit(solution)/shard_map/ppermute | solution.py:187

commit v2 on v1

--- a/solution.py
+++ b/solution.py
@@ -31,28 +31,36 @@
     return jnp.where(seen, 0.0, NEG).astype(jnp.float32)
 
 
-def mass_call(own_queries, sibling_queries, keys, order, bias, scale, factor):
-    half, _, per_group, head_dim = own_queries.shape
+def scaled_parts(values, scale):
+    scaled = values.astype(jnp.float32) * scale
+    upper = lax.reduce_precision(scaled, exponent_bits=8, mantissa_bits=7)
+    return [upper.astype(jnp.bfloat16), (scaled - upper).astype(jnp.bfloat16)]
+
+
+def mass_call(query_parts, keys, order, bias, factor):
+    half, _, per_group, head_dim = query_parts[0].shape
     chunks = len(keys)
     groups, local_keys, _ = keys[0].shape
     total = chunks * local_keys
     step = max(8, min(half, (1 << 20) // (per_group * total)))
 
-    def kernel(own_ref, sibling_ref, *refs):
-        key_refs, bias_ref, out_ref, all_keys = refs[:chunks], refs[chunks], refs[-2], refs[-1]
-        sub = lax.axis_index("sub")
+    def kernel(*refs):
+        query_refs, refs = refs[:4], refs[4:]
+        key_refs, bias_ref, out_ref = refs[:chunks], refs[chunks], refs[-1]
         ctx = lax.axis_index("ctx")
-        for index, key_ref in enumerate(key_refs):
-            all_keys[:, index * local_keys : (index + 1) * local_keys, :] = key_ref[...]
         for group in range(groups):
-            block_keys = all_keys[group]
+            block_keys = jnp.concatenate([key_ref[group] for key_ref in key_refs], axis=0)
+            block_keys = jnp.concatenate([block_keys, block_keys], axis=1)
             mass = jnp.zeros((per_group, total), jnp.float32)
-            for part, query_ref in enumerate((own_ref, sibling_ref)):
+            for part in range(2):
 
                 def advance(index, mass):
-                    rows = query_ref[pl.ds(index * step, step), part * (sub * groups) + group]
+                    rows = [
+                        query_ref[pl.ds(index * step, step), group].reshape(-1, head_dim)
+                        for query_ref in query_refs[2 * part : 2 * part + 2]
+                    ]
                     scores = lax.dot_general(
-                        rows.reshape(step * per_group, head_dim),
+                        jnp.concatenate(rows, axis=1),
                         block_keys,
                         (((1,), (1,)), ((), ())),
                         preferred_element_type=jnp.float32,
@@ -68,7 +76,7 @@
                         hidden = bias_ref[pl.ds(first, step), :][:, None, :]
                     scores = scores + hidden
                     peak = jnp.max(scores, axis=-1, keepdims=True)
-                    terms = jnp.exp2((scores - peak) * (scale * LOG2E))
+                    terms = jnp.exp2(scores - peak)
                     weight = 1.0 / jnp.sum(terms, axis=-1, keepdims=True)
                     return mass + jnp.sum(terms * weight, axis=0)
 
@@ -86,16 +94,15 @@
     return pl.pallas_call(
         kernel,
         out_shape=jax.ShapeDtypeStruct((groups * chunks, local_keys), jnp.float32),
-        in_specs=[VMEM] * (3 + chunks),
+        in_specs=[VMEM] * (5 + chunks),
         out_specs=VMEM,
-        scratch_shapes=[pltpu.VMEM((groups, total, head_dim), jnp.bfloat16)],
         compiler_params=pltpu.CompilerParams(vmem_limit_bytes=32 << 20),
         cost_estimate=pl.CostEstimate(
             flops=4 * half * per_group * groups * total * head_dim,
             bytes_accessed=1 << 20,
             transcendentals=2 * half * per_group * groups * total,
         ),
-    )(own_queries, sibling_queries, *keys, bias)
+    )(*query_parts, *keys, bias)
 
 
 def finish_call(mine, theirs, edges, groups, chunks):
@@ -172,8 +179,11 @@
     owners = jnp.bitwise_xor(ctx, jnp.array([0, *order], jnp.int32))
     bias = visible_bias(positions, lists, owners, local_keys)
 
-    own_queries = lax.dynamic_slice_in_dim(queries4, sub * groups, groups, 1)
-    mass = mass_call(own_queries, sibling_queries, keys, order, bias, scale, factor)
+    query_parts = []
+    for part in (queries4, sibling_queries):
+        part = lax.dynamic_slice_in_dim(part, sub * groups, groups, 1)
+        query_parts += scaled_parts(part, scale * LOG2E)
+    mass = mass_call(query_parts, keys, order, bias, factor)
 
     near = lax.ppermute(mass, "ctx", xor_pairs(ctx_count, 1))
     aside = lax.ppermute(mass, "sub", swap)

time: 25.6 us -> 25.1 us (0.980)
  other arithmetic: 0.49 us -> 1.95 us
  local copies, waits for them, and re-layouts: 3.47 us -> 2.4 us
  waiting for transfers between devices: 6.98 us -> 6.51 us
  starting transfers between devices: 10.4 us -> 10.1 us
    ppermute x1, waiting for transfers between devices: 3.12 us -> 1.39 us  [local(): near = lax.ppermute(mass, 'ctx', xor_pairs(ctx_count, 1))]
    convert_element_type x0 -> x2, other arithmetic: none -> 1.46 us  [scaled_parts(): return [upper.astype(jnp.bfloat16), (scaled - upper).astype(jnp.bfloat16)]]
    ppermute x1, starting transfers between devices: 0.41 us -> 1.86 us  [local(): near = lax.ppermute(mass, 'ctx', xor_pairs(ctx_count, 1))]
    ppermute x1, starting transfers between devices: 1.71 us -> 0.34 us  [local(): across = lax.ppermute(mass, ('ctx', 'sub'), xor_pairs(both_count, 3))]
    ppermute x1, waiting for transfers between devices: 0.01 us -> 1.22 us  [local(): across = lax.ppermute(mass, ('ctx', 'sub'), xor_pairs(both_count, 3))]
    dynamic_slice x1 -> x0, local copies, waits for them, and re-layouts: 1.08 us -> none  [local(): own_queries = lax.dynamic_slice_in_dim(queries4, sub * groups, groups, 1)]
    ppermute x1, starting transfers between devices: 2.01 us -> 1.69 us  [local(): theirs = lax.ppermute(mine, 'ctx', xor_pairs(ctx_count, distance))]
  transfers between devices with their start and end apart: 10 -> 10, of which waited for: 5 -> 4; matrix products, arithmetic and copies ran while one was open for 7% -> 8% of each run, Pallas kernels for 0% -> 0%
where the time goes in v2:
time: 25.1 us; the launch traced here: 24.9 us
  starting transfers between devices  10.1 us (40%)
  waiting for transfers between devices  6.51 us (26%)
  Pallas kernels  3.12 us (12%)
  local copies, waits for them, and re-layouts  2.4 us (10%)
  other arithmetic  1.95 us (8%)
  between operations  0.77 us (3%)
    ppermute x3, starting transfers between devices, local(): lax.ppermute(own_keys, 'ctx', xor_pairs(ctx_count, distance))  5.71 us
    ppermute x1, waiting for transfers between devices, local(): theirs = lax.ppermute(mine, 'ctx', xor_pairs(ctx_count, distance))  2.85 us
    pallas_call x1, Pallas kernels, mass_call(): pl.pallas_call(kernel, out_shape=jax.ShapeDtypeStruct((groups * chunks, l...  2.36 us
    unnamed x12, local copies, waits for them, and re-layouts  2.24 us
    ppermute x1, starting transfers between devices, local(): near = lax.ppermute(mass, 'ctx', xor_pairs(ctx_count, 1))  1.86 us
    ppermute x1, starting transfers between devices, local(): theirs = lax.ppermute(mine, 'ctx', xor_pairs(ctx_count, distance))  1.69 us
    convert_element_type x2, other arithmetic, scaled_parts(): return [upper.astype(jnp.bfloat16), (scaled - upper).astype(jnp.bfloat16)]  1.46 us
    ppermute x1, waiting for transfers between devices, local(): near = lax.ppermute(mass, 'ctx', xor_pairs(ctx_count, 1))  1.39 us
  transfers between devices with their start and end apart: 10, of which 4 were waited for; matrix products, arithmetic and copies ran while one was open for 8% of the time, Pallas kernels for 0%

profile of v2, /device:TPU:0, one launch (start us, length us, event | category | flops | bytes accessed | tf_op | source)
XLA Modules:
  0.0 24.9 jit_solution(8978091280834982526)
XLA Ops:
  0.7 0.9 %copy-done = bf16[128,4,128]{2,1,0:T(4,128)(2,1)S(1)} copy-done((bf16[128,4,128]{2,1,0:T(4,128)(2,1)S(1)}, bf16[128,4,128]{2,1,0:T(4,128)(2,1)}, u32[]{:S(2)}) %copy-start) | copy-done | bytes 131096
  1.5 0.1 constant_dynamic-slice_fusion
  1.6 4.1 %collective-permute-start.1 = (bf16[2,128,128]{2,1,0:T(8,128)(2,1)S(1)}, bf16[2,128,128]{2,1,0:T(8,128)(2,1)S(1)}, u32[]{:S(2)}, u32[]{:S(2)}) collective-permute-start(bf16[2,128,128]{2,1,0:T(8,128)(2,1)S(1)} %bitcast.34), channel_id=1, source_target_pairs={{0,8},{4,12},{8,0},{12,4},{1,9},{5,13},{9,1},{13,5},{2,10},{6,14},... | collective-permute-start | bytes 196616 | tf_op jit(solution)/shard_map/ppermute | solution.py:170
  5.8 1.3 %collective-permute-start.2 = (bf16[2,128,128]{2,1,0:T(8,128)(2,1)S(1)}, bf16[2,128,128]{2,1,0:T(8,128)(2,1)S(1)}, u32[]{:S(2)}, u32[]{:S(2)}) collective-permute-start(bf16[2,128,128]{2,1,0:T(8,128)(2,1)S(1)} %bitcast.35), channel_id=1, source_target_pairs={{0,12},{4,8},{8,4},{12,0},{1,13},{5,9},{9,5},{13,1},{2,14},{6,10},... | collective-permute-start | bytes 196616 | tf_op jit(solution)/shard_map/ppermute | solution.py:170
  7.1 0.2 collective-permute-start.3
  7.4 0.5 %collective-permute-start.5 = (s32[1,8]{1,0:T(1,128)S(1)}, s32[1,8]{1,0:T(1,128)S(1)}, u32[]{:S(2)}, u32[]{:S(2)}) collective-permute-start(s32[1,8]{1,0:T(1,128)S(1)} %copy-done.2), channel_id=1, source_target_pairs={{0,1},{1,0},{2,3},{3,2},{4,5},{5,4},{6,7},{7,6},{8,9},{9,8},{10,11... | collective-permute-start | bytes 104 | tf_op jit(solution)/shard_map/ppermute | solution.py:178
  7.9 1.2 %fusion = (bf16[128,2,8,128]{3,2,1,0:T(8,128)(2,1)S(1)}, bf16[128,2,8,128]{3,2,1,0:T(8,128)(2,1)S(1)}) fusion(bf16[128,4,8,128]{3,2,1,0:T(8,128)(2,1)} %bitcast.39, s32[]{:T(128)S(6)} %select_n.31), kind=kLoop, calls=%fused_computation.4 | loop fusion | flops 1572864 | bytes 1572868 | tf_op jit(solution)/shard_map/convert_element_type | solution.py:37
  9.1 0.6 %copy-done.4 = s32[4]{0:T(128)S(1)} copy-done((s32[4]{0:T(128)S(1)}, s32[4]{0:T(128)}, u32[]{:S(2)}) %copy-start.4) | copy-done | bytes 40
  9.8 0.6 %copy-done.3 = s32[128]{0:T(128)S(1)} copy-done((s32[128]{0:T(128)S(1)}, s32[128]{0:T(128)}, u32[]{:S(2)}) %copy-start.3) | copy-done | bytes 536
  10.5 0.1 add_select_fusion
  10.5 0.1 add_bitcast_fusion
  10.7 0.1 compare_reduce_fusion
  10.7 1.0 %collective-permute-done.4 = s32[128]{0:T(128)S(1)} collective-permute-done((s32[128]{0:T(128)S(1)}, s32[128]{0:T(128)S(1)}, u32[]{:S(2)}, u32[]{:S(2)}) %collective-permute-start.4) | collective-permute-done | bytes 544 | tf_op jit(solution)/shard_map/ppermute | solution.py:177
  11.8 0.2 fusion.3.refs_8_
  12.0 0.2 fusion.1
  12.3 2.4 %shard_map.77 = f32[8,128]{1,0:T(8,128)S(1)} custom-call(bf16[128,2,8,128]{3,2,1,0:T(8,128)(2,1)S(1)} %get-tuple-element.5.refs_0_, bf16[128,2,8,128]{3,2,1,0:T(8,128)(2,1)S(1)} %get-tuple-element.4.refs_1_, bf16[128,2,8,128]{3,2,1,0:T(8,128)(2,1)S(1)} %get-tuple-element.3.refs_2_, bf16[128,2,8,128]{3,2,1,0:T(8,128)(2,1)S(1)} %get-tuple-element.2.refs_3_, ...), custom_call_target="tpu_custom_call" | custom-call | flops 536870912 | bytes 1048576 | tf_op jit(solution)/shard_map/pallas_call | solution.py:94
  14.7 1.9 %collective-permute-start.6 = (f32[8,128]{1,0:T(8,128)S(1)}, f32[8,128]{1,0:T(8,128)S(1)}, u32[]{:S(2)}, u32[]{:S(2)}) collective-permute-start(f32[8,128]{1,0:T(8,128)S(1)} %shard_map.77), channel_id=1, source_target_pairs={{0,4},{4,0},{8,12},{12,8},{1,5},{5,1},{9,13},{13,9},{2,6},{6,2},{1... | collective-permute-start | bytes 12296 | tf_op jit(solution)/shard_map/ppermute | solution.py:188
  16.5 0.3 %collective-permute-start.8 = (f32[8,128]{1,0:T(8,128)S(1)}, f32[8,128]{1,0:T(8,128)S(1)}, u32[]{:S(2)}, u32[]{:S(2)}) collective-permute-start(f32[8,128]{1,0:T(8,128)S(1)} %shard_map.77), channel_id=1, source_target_pairs={{0,5},{1,4},{4,1},{5,0},{8,13},{9,12},{12,9},{13,8},{2,7},{3,6},{6... | collective-permute-start | bytes 12296 | tf_op jit(solution)/shard_map/ppermute | solution.py:190
  16.9 0.1 slice_bitcast_fusion.1
  17.0 1.4 %collective-permute-done.6 = f32[8,128]{1,0:T(8,128)S(1)} collective-permute-done((f32[8,128]{1,0:T(8,128)S(1)}, f32[8,128]{1,0:T(8,128)S(1)}, u32[]{:S(2)}, u32[]{:S(2)}) %collective-permute-start.6) | collective-permute-done | bytes 4128 | tf_op jit(solution)/shard_map/ppermute | solution.py:188
  18.4 1.2 %collective-permute-done.8 = f32[8,128]{1,0:T(8,128)S(1)} collective-permute-done((f32[8,128]{1,0:T(8,128)S(1)}, f32[8,128]{1,0:T(8,128)S(1)}, u32[]{:S(2)}, u32[]{:S(2)}) %collective-permute-start.8) | collective-permute-done | bytes 4128 | tf_op jit(solution)/shard_map/ppermute | solution.py:190
  19.6 1.7 %collective-permute-start.9 = (f32[16,128]{1,0:T(8,128)S(1)}, f32[16,128]{1,0:T(8,128)S(1)}, u32[]{:S(2)}, u32[]{:S(2)}) collective-permute-start(f32[16,128]{1,0:T(8,128)S(1)} %pad_maximum_fusion.mine_ref), channel_id=1, source_target_pairs={{0,8},{4,12},{8,0},{12,4},{1,9},{5,13},{9,1},{13,5},{2,10},{6,14},... | collective-permute-start | bytes 24584 | tf_op jit(solution)/shard_map/ppermute | solution.py:197
  21.3 2.8 %collective-permute-done.9.theirs_ref = f32[16,128]{1,0:T(8,128)S(1)} collective-permute-done((f32[16,128]{1,0:T(8,128)S(1)}, f32[16,128]{1,0:T(8,128)S(1)}, u32[]{:S(2)}, u32[]{:S(2)}) %collective-permute-start.9) | collective-permute-done | bytes 8224 | tf_op jit(solution)/shard_map/ppermute | solution.py:197
  24.1 0.8 %shard_map.78 = (f32[4,128]{1,0:T(4,128)}, f32[4,128]{1,0:T(4,128)}) custom-call(f32[16,128]{1,0:T(8,128)S(1)} %pad_maximum_fusion.mine_ref, f32[16,128]{1,0:T(8,128)S(1)} %collective-permute-done.9.theirs_ref, s32[2,128]{1,0:T(2,128)S(1)} %pad_add_fusion.1.edges_ref), custom_call_target="tpu_custom_call" | custom-call | tf_op jit(solution)/shard_map/pallas_call | solution.py:140
  (27 shorter events, 0.1 us)
Async XLA Ops:
  0.6 0.9 %copy-start = (bf16[128,4,128]{2,1,0:T(4,128)(2,1)S(1)}, bf16[128,4,128]{2,1,0:T(4,128)(2,1)}, u32[]{:S(2)}) copy-start(bf16[128,4,128]{2,1,0:T(4,128)(2,1)} %param.7) | copy-start | bytes 393220
  1.6 5.7 %copy-start.2 = (s32[1,8]{1,0:T(1,128)S(1)}, s32[1,8]{1,0:T(1,128)}, u32[]{:S(2)}) copy-start(s32[1,8]{1,0:T(1,128)} %param.9) | copy-start | bytes 100
  1.6 10.6 %collective-permute-start.1 = (bf16[2,128,128]{2,1,0:T(8,128)(2,1)S(1)}, bf16[2,128,128]{2,1,0:T(8,128)(2,1)S(1)}, u32[]{:S(2)}, u32[]{:S(2)}) collective-permute-start(bf16[2,128,128]{2,1,0:T(8,128)(2,1)S(1)} %bitcast.34), channel_id=1, source_target_pairs={{0,8},{4,12},{8,0},{12,4},{1,9},{5,13},{9,1},{13,5},{2,10},{6,14},... | collective-permute-start | bytes 196616 | tf_op jit(solution)/shard_map/ppermute | solution.py:170
  5.8 6.5 %collective-permute-start.2 = (bf16[2,128,128]{2,1,0:T(8,128)(2,1)S(1)}, bf16[2,128,128]{2,1,0:T(8,128)(2,1)S(1)}, u32[]{:S(2)}, u32[]{:S(2)}) collective-permute-start(bf16[2,128,128]{2,1,0:T(8,128)(2,1)S(1)} %bitcast.35), channel_id=1, source_target_pairs={{0,12},{4,8},{8,4},{12,0},{1,13},{5,9},{9,5},{13,1},{2,14},{6,10},... | collective-permute-start | bytes 196616 | tf_op jit(solution)/shard_map/ppermute | solution.py:170
  7.1 5.2 %collective-permute-start.3 = (bf16[2,128,128]{2,1,0:T(8,128)(2,1)S(1)}, bf16[2,128,128]{2,1,0:T(8,128)(2,1)S(1)}, u32[]{:S(2)}, u32[]{:S(2)}) collective-permute-start(bf16[2,128,128]{2,1,0:T(8,128)(2,1)S(1)} %bitcast.36), channel_id=1, source_target_pairs={{0,4},{4,0},{8,12},{12,8},{1,5},{5,1},{9,13},{13,9},{2,6},{6,2},{1... | collective-permute-start | bytes 196616 | tf_op jit(solution)/shard_map/ppermute | solution.py:170
  7.4 4.7 %collective-permute-start = (bf16[128,4,8,128]{3,2,1,0:T(8,128)(2,1)}, bf16[128,4,8,128]{3,2,1,0:T(8,128)(2,1)S(1)}, u32[]{:S(2)}, u32[]{:S(2)}) collective-permute-start(bf16[128,4,8,128]{3,2,1,0:T(8,128)(2,1)} %bitcast.38), channel_id=1, source_target_pairs={{0,1},{1,0},{2,3},{3,2},{4,5},{5,4},{6,7},{7,6},{8,9},{9,8},{10,11... | collective-permute-start | bytes 3145736 | tf_op jit(solution)/shard_map/ppermute | solution.py:176
  7.4 3.3 %collective-permute-start.5 = (s32[1,8]{1,0:T(1,128)S(1)}, s32[1,8]{1,0:T(1,128)S(1)}, u32[]{:S(2)}, u32[]{:S(2)}) collective-permute-start(s32[1,8]{1,0:T(1,128)S(1)} %copy-done.2), channel_id=1, source_target_pairs={{0,1},{1,0},{2,3},{3,2},{4,5},{5,4},{6,7},{7,6},{8,9},{9,8},{10,11... | collective-permute-start | bytes 104 | tf_op jit(solution)/shard_map/ppermute | solution.py:178
  9.1 0.7 %copy-start.4 = (s32[4]{0:T(128)S(1)}, s32[4]{0:T(128)}, u32[]{:S(2)}) copy-start(s32[4]{0:T(128)} %constant.51.clone) | copy-start | bytes 52
  9.8 0.7 %copy-start.3 = (s32[128]{0:T(128)S(1)}, s32[128]{0:T(128)}, u32[]{:S(2)}) copy-start(s32[128]{0:T(128)} %param.8) | copy-start | bytes 1540
  10.6 1.2 %collective-permute-start.4 = (s32[128]{0:T(128)S(1)}, s32[128]{0:T(128)S(1)}, u32[]{:S(2)}, u32[]{:S(2)}) collective-permute-start(s32[128]{0:T(128)S(1)} %copy-done.3), channel_id=1, source_target_pairs={{0,1},{1,0},{2,3},{3,2},{4,5},{5,4},{6,7},{7,6},{8,9},{9,8},{10,11... | collective-permute-start | bytes 1544 | tf_op jit(solution)/shard_map/ppermute | solution.py:177
  12.3 4.6 %copy-start.1 = (s32[129]{0:T(256)S(1)}, s32[129]{0:T(256)}, u32[]{:S(2)}) copy-start(s32[129]{0:T(256)} %param.10) | copy-start | bytes 1552
  14.7 3.7 %collective-permute-start.6 = (f32[8,128]{1,0:T(8,128)S(1)}, f32[8,128]{1,0:T(8,128)S(1)}, u32[]{:S(2)}, u32[]{:S(2)}) collective-permute-start(f32[8,128]{1,0:T(8,128)S(1)} %shard_map.77), channel_id=1, source_target_pairs={{0,4},{4,0},{8,12},{12,8},{1,5},{5,1},{9,13},{13,9},{2,6},{6,2},{1... | collective-permute-start | bytes 12296 | tf_op jit(solution)/shard_map/ppermute | solution.py:188
  16.5 1.8 %collective-permute-start.7 = (f32[8,128]{1,0:T(8,128)S(1)}, f32[8,128]{1,0:T(8,128)S(1)}, u32[]{:S(2)}, u32[]{:S(2)}) collective-permute-start(f32[8,128]{1,0:T(8,128)S(1)} %shard_map.77), channel_id=1, source_target_pairs={{0,1},{1,0},{2,3},{3,2},{4,5},{5,4},{6,7},{7,6},{8,9},{9,8},{10,11... | collective-permute-start | bytes 12296 | tf_op jit(solution)/shard_map/ppermute | solution.py:189
  16.5 3.0 %collective-permute-start.8 = (f32[8,128]{1,0:T(8,128)S(1)}, f32[8,128]{1,0:T(8,128)S(1)}, u32[]{:S(2)}, u32[]{:S(2)}) collective-permute-start(f32[8,128]{1,0:T(8,128)S(1)} %shard_map.77), channel_id=1, source_target_pairs={{0,5},{1,4},{4,1},{5,0},{8,13},{9,12},{12,9},{13,8},{2,7},{3,6},{6... | collective-permute-start | bytes 12296 | tf_op jit(solution)/shard_map/ppermute | solution.py:190
  19.6 4.5 %collective-permute-start.9 = (f32[16,128]{1,0:T(8,128)S(1)}, f32[16,128]{1,0:T(8,128)S(1)}, u32[]{:S(2)}, u32[]{:S(2)}) collective-permute-start(f32[16,128]{1,0:T(8,128)S(1)} %pad_maximum_fusion.mine_ref), channel_id=1, source_target_pairs={{0,8},{4,12},{8,0},{12,4},{1,9},{5,13},{9,1},{13,5},{2,10},{6,14},... | collective-permute-start | bytes 24584 | tf_op jit(solution)/shard_map/ppermute | solution.py:197

commit v3 on v2

--- a/solution.py
+++ b/solution.py
@@ -116,7 +116,8 @@
         for part in range(2):
             place = jnp.bitwise_xor(sub, part) * half
             rows_here = slice(part * half, (part + 1) * half)
-            total[pl.ds(place, half), :] = mine_ref[rows_here, :] + theirs_ref[rows_here, :]
+            swapped = slice((1 - part) * half, (2 - part) * half)
+            total[pl.ds(place, half), :] = mine_ref[rows_here, :] + theirs_ref[swapped, :]
         low, high = edges_ref[0:1, :], edges_ref[1:2, :]
         sums = jnp.zeros((2 * groups * 3, bins), jnp.float32)
         for chunk in range(chunks):
@@ -194,7 +195,9 @@
     while distance < ctx_count:
         if theirs is not None:
             mine = mine + theirs
-        theirs = lax.ppermute(mine, "ctx", xor_pairs(ctx_count, distance))
+        last = distance * 2 >= ctx_count
+        pairs = xor_pairs(both_count, distance * sub_count + (1 if last else 0))
+        theirs = lax.ppermute(mine, ("ctx", "sub"), pairs)
         distance *= 2
     edges = jnp.stack([bin_edges[:-1], bin_edges[1:]])
     return finish_call(mine, theirs, edges, groups, ctx_count)

time: 25.1 us -> 24.5 us (0.976)
  waiting for transfers between devices: 6.51 us -> 5.83 us
    ppermute x1, waiting for transfers between devices: 2.85 us -> 2.16 us  [local(): theirs = lax.ppermute(mine, ('ctx', 'sub'), pairs)]
where the time goes in v3:
time: 24.5 us; the launch traced here: 24.3 us
  starting transfers between devices  10.2 us (42%)
  waiting for transfers between devices  5.83 us (24%)
  Pallas kernels  3.12 us (13%)
  local copies, waits for them, and re-layouts  2.4 us (10%)
  other arithmetic  1.95 us (8%)
  between operations  0.77 us (3%)
    ppermute x3, starting transfers between devices, local(): lax.ppermute(own_keys, 'ctx', xor_pairs(ctx_count, distance))  5.71 us
    pallas_call x1, Pallas kernels, mass_call(): pl.pallas_call(kernel, out_shape=jax.ShapeDtypeStruct((groups * chunks, l...  2.36 us
    unnamed x12, local copies, waits for them, and re-layouts  2.24 us
    ppermute x1, waiting for transfers between devices, local(): theirs = lax.ppermute(mine, ('ctx', 'sub'), pairs)  2.16 us
    ppermute x1, starting transfers between devices, local(): near = lax.ppermute(mass, 'ctx', xor_pairs(ctx_count, 1))  1.86 us
    ppermute x1, starting transfers between devices, local(): theirs = lax.ppermute(mine, ('ctx', 'sub'), pairs)  1.8 us
    convert_element_type x2, other arithmetic, scaled_parts(): return [upper.astype(jnp.bfloat16), (scaled - upper).astype(jnp.bfloat16)]  1.46 us
    ppermute x1, waiting for transfers between devices, local(): near = lax.ppermute(mass, 'ctx', xor_pairs(ctx_count, 1))  1.39 us
  transfers between devices with their start and end apart: 10, of which 4 were waited for; matrix products, arithmetic and copies ran while one was open for 8% of the time, Pallas kernels for 0%

profile of v3, /device:TPU:0, one launch (start us, length us, event | category | flops | bytes accessed | tf_op | source)
XLA Modules:
  0.0 24.3 jit_solution(14779867155216560005)
XLA Ops:
  0.7 0.9 %copy-done = bf16[128,4,128]{2,1,0:T(4,128)(2,1)S(1)} copy-done((bf16[128,4,128]{2,1,0:T(4,128)(2,1)S(1)}, bf16[128,4,128]{2,1,0:T(4,128)(2,1)}, u32[]{:S(2)}) %copy-start) | copy-done | bytes 131096
  1.5 0.1 constant_dynamic-slice_fusion
  1.6 4.1 %collective-permute-start.1 = (bf16[2,128,128]{2,1,0:T(8,128)(2,1)S(1)}, bf16[2,128,128]{2,1,0:T(8,128)(2,1)S(1)}, u32[]{:S(2)}, u32[]{:S(2)}) collective-permute-start(bf16[2,128,128]{2,1,0:T(8,128)(2,1)S(1)} %bitcast.34), channel_id=1, source_target_pairs={{0,8},{4,12},{8,0},{12,4},{1,9},{5,13},{9,1},{13,5},{2,10},{6,14},... | collective-permute-start | bytes 196616 | tf_op jit(solution)/shard_map/ppermute | solution.py:171
  5.8 1.3 %collective-permute-start.2 = (bf16[2,128,128]{2,1,0:T(8,128)(2,1)S(1)}, bf16[2,128,128]{2,1,0:T(8,128)(2,1)S(1)}, u32[]{:S(2)}, u32[]{:S(2)}) collective-permute-start(bf16[2,128,128]{2,1,0:T(8,128)(2,1)S(1)} %bitcast.35), channel_id=1, source_target_pairs={{0,12},{4,8},{8,4},{12,0},{1,13},{5,9},{9,5},{13,1},{2,14},{6,10},... | collective-permute-start | bytes 196616 | tf_op jit(solution)/shard_map/ppermute | solution.py:171
  7.1 0.2 collective-permute-start.3
  7.4 0.5 %collective-permute-start.5 = (s32[1,8]{1,0:T(1,128)S(1)}, s32[1,8]{1,0:T(1,128)S(1)}, u32[]{:S(2)}, u32[]{:S(2)}) collective-permute-start(s32[1,8]{1,0:T(1,128)S(1)} %copy-done.2), channel_id=1, source_target_pairs={{0,1},{1,0},{2,3},{3,2},{4,5},{5,4},{6,7},{7,6},{8,9},{9,8},{10,11... | collective-permute-start | bytes 104 | tf_op jit(solution)/shard_map/ppermute | solution.py:179
  7.9 1.2 %fusion = (bf16[128,2,8,128]{3,2,1,0:T(8,128)(2,1)S(1)}, bf16[128,2,8,128]{3,2,1,0:T(8,128)(2,1)S(1)}) fusion(bf16[128,4,8,128]{3,2,1,0:T(8,128)(2,1)} %bitcast.39, s32[]{:T(128)S(6)} %select_n.31), kind=kLoop, calls=%fused_computation.4 | loop fusion | flops 1572864 | bytes 1572868 | tf_op jit(solution)/shard_map/convert_element_type | solution.py:37
  9.1 0.6 %copy-done.4 = s32[4]{0:T(128)S(1)} copy-done((s32[4]{0:T(128)S(1)}, s32[4]{0:T(128)}, u32[]{:S(2)}) %copy-start.4) | copy-done | bytes 40
  9.8 0.6 %copy-done.3 = s32[128]{0:T(128)S(1)} copy-done((s32[128]{0:T(128)S(1)}, s32[128]{0:T(128)}, u32[]{:S(2)}) %copy-start.3) | copy-done | bytes 536
  10.5 0.1 add_select_fusion
  10.5 0.1 add_bitcast_fusion
  10.7 0.1 compare_reduce_fusion
  10.7 1.0 %collective-permute-done.4 = s32[128]{0:T(128)S(1)} collective-permute-done((s32[128]{0:T(128)S(1)}, s32[128]{0:T(128)S(1)}, u32[]{:S(2)}, u32[]{:S(2)}) %collective-permute-start.4) | collective-permute-done | bytes 544 | tf_op jit(solution)/shard_map/ppermute | solution.py:178
  11.8 0.2 fusion.3.refs_8_
  12.0 0.2 fusion.1
  12.3 2.4 %shard_map.77 = f32[8,128]{1,0:T(8,128)S(1)} custom-call(bf16[128,2,8,128]{3,2,1,0:T(8,128)(2,1)S(1)} %get-tuple-element.5.refs_0_, bf16[128,2,8,128]{3,2,1,0:T(8,128)(2,1)S(1)} %get-tuple-element.4.refs_1_, bf16[128,2,8,128]{3,2,1,0:T(8,128)(2,1)S(1)} %get-tuple-element.3.refs_2_, bf16[128,2,8,128]{3,2,1,0:T(8,128)(2,1)S(1)} %get-tuple-element.2.refs_3_, ...), custom_call_target="tpu_custom_call" | custom-call | flops 536870912 | bytes 1048576 | tf_op jit(solution)/shard_map/pallas_call | solution.py:94
  14.7 1.9 %collective-permute-start.6 = (f32[8,128]{1,0:T(8,128)S(1)}, f32[8,128]{1,0:T(8,128)S(1)}, u32[]{:S(2)}, u32[]{:S(2)}) collective-permute-start(f32[8,128]{1,0:T(8,128)S(1)} %shard_map.77), channel_id=1, source_target_pairs={{0,4},{4,0},{8,12},{12,8},{1,5},{5,1},{9,13},{13,9},{2,6},{6,2},{1... | collective-permute-start | bytes 12296 | tf_op jit(solution)/shard_map/ppermute | solution.py:189
  16.5 0.3 %collective-permute-start.8 = (f32[8,128]{1,0:T(8,128)S(1)}, f32[8,128]{1,0:T(8,128)S(1)}, u32[]{:S(2)}, u32[]{:S(2)}) collective-permute-start(f32[8,128]{1,0:T(8,128)S(1)} %shard_map.77), channel_id=1, source_target_pairs={{0,5},{1,4},{4,1},{5,0},{8,13},{9,12},{12,9},{13,8},{2,7},{3,6},{6... | collective-permute-start | bytes 12296 | tf_op jit(solution)/shard_map/ppermute | solution.py:191
  16.9 0.1 slice_bitcast_fusion.1
  17.0 1.4 %collective-permute-done.6 = f32[8,128]{1,0:T(8,128)S(1)} collective-permute-done((f32[8,128]{1,0:T(8,128)S(1)}, f32[8,128]{1,0:T(8,128)S(1)}, u32[]{:S(2)}, u32[]{:S(2)}) %collective-permute-start.6) | collective-permute-done | bytes 4128 | tf_op jit(solution)/shard_map/ppermute | solution.py:189
  18.4 1.2 %collective-permute-done.8 = f32[8,128]{1,0:T(8,128)S(1)} collective-permute-done((f32[8,128]{1,0:T(8,128)S(1)}, f32[8,128]{1,0:T(8,128)S(1)}, u32[]{:S(2)}, u32[]{:S(2)}) %collective-permute-start.8) | collective-permute-done | bytes 4128 | tf_op jit(solution)/shard_map/ppermute | solution.py:191
  19.6 1.8 %collective-permute-start.9 = (f32[16,128]{1,0:T(8,128)S(1)}, f32[16,128]{1,0:T(8,128)S(1)}, u32[]{:S(2)}, u32[]{:S(2)}) collective-permute-start(f32[16,128]{1,0:T(8,128)S(1)} %pad_maximum_fusion.mine_ref), channel_id=1, source_target_pairs={{0,9},{1,8},{4,13},{5,12},{8,1},{9,0},{12,5},{13,4},{2,11},{3,10},... | collective-permute-start | bytes 24584 | tf_op jit(solution)/shard_map/ppermute | solution.py:200
  21.4 2.2 %collective-permute-done.9.theirs_ref = f32[16,128]{1,0:T(8,128)S(1)} collective-permute-done((f32[16,128]{1,0:T(8,128)S(1)}, f32[16,128]{1,0:T(8,128)S(1)}, u32[]{:S(2)}, u32[]{:S(2)}) %collective-permute-start.9) | collective-permute-done | bytes 8224 | tf_op jit(solution)/shard_map/ppermute | solution.py:200
  23.6 0.8 %shard_map.78 = (f32[4,128]{1,0:T(4,128)}, f32[4,128]{1,0:T(4,128)}) custom-call(f32[16,128]{1,0:T(8,128)S(1)} %pad_maximum_fusion.mine_ref, f32[16,128]{1,0:T(8,128)S(1)} %collective-permute-done.9.theirs_ref, s32[2,128]{1,0:T(2,128)S(1)} %pad_add_fusion.1.edges_ref), custom_call_target="tpu_custom_call" | custom-call | tf_op jit(solution)/shard_map/pallas_call | solution.py:141
  (27 shorter events, 0.1 us)
Async XLA Ops:
  0.6 0.9 %copy-start = (bf16[128,4,128]{2,1,0:T(4,128)(2,1)S(1)}, bf16[128,4,128]{2,1,0:T(4,128)(2,1)}, u32[]{:S(2)}) copy-start(bf16[128,4,128]{2,1,0:T(4,128)(2,1)} %param.7) | copy-start | bytes 393220
  1.6 5.7 %copy-start.2 = (s32[1,8]{1,0:T(1,128)S(1)}, s32[1,8]{1,0:T(1,128)}, u32[]{:S(2)}) copy-start(s32[1,8]{1,0:T(1,128)} %param.9) | copy-start | bytes 100
  1.6 10.6 %collective-permute-start.1 = (bf16[2,128,128]{2,1,0:T(8,128)(2,1)S(1)}, bf16[2,128,128]{2,1,0:T(8,128)(2,1)S(1)}, u32[]{:S(2)}, u32[]{:S(2)}) collective-permute-start(bf16[2,128,128]{2,1,0:T(8,128)(2,1)S(1)} %bitcast.34), channel_id=1, source_target_pairs={{0,8},{4,12},{8,0},{12,4},{1,9},{5,13},{9,1},{13,5},{2,10},{6,14},... | collective-permute-start | bytes 196616 | tf_op jit(solution)/shard_map/ppermute | solution.py:171
  5.8 6.5 %collective-permute-start.2 = (bf16[2,128,128]{2,1,0:T(8,128)(2,1)S(1)}, bf16[2,128,128]{2,1,0:T(8,128)(2,1)S(1)}, u32[]{:S(2)}, u32[]{:S(2)}) collective-permute-start(bf16[2,128,128]{2,1,0:T(8,128)(2,1)S(1)} %bitcast.35), channel_id=1, source_target_pairs={{0,12},{4,8},{8,4},{12,0},{1,13},{5,9},{9,5},{13,1},{2,14},{6,10},... | collective-permute-start | bytes 196616 | tf_op jit(solution)/shard_map/ppermute | solution.py:171
  7.1 5.2 %collective-permute-start.3 = (bf16[2,128,128]{2,1,0:T(8,128)(2,1)S(1)}, bf16[2,128,128]{2,1,0:T(8,128)(2,1)S(1)}, u32[]{:S(2)}, u32[]{:S(2)}) collective-permute-start(bf16[2,128,128]{2,1,0:T(8,128)(2,1)S(1)} %bitcast.36), channel_id=1, source_target_pairs={{0,4},{4,0},{8,12},{12,8},{1,5},{5,1},{9,13},{13,9},{2,6},{6,2},{1... | collective-permute-start | bytes 196616 | tf_op jit(solution)/shard_map/ppermute | solution.py:171
  7.4 4.7 %collective-permute-start = (bf16[128,4,8,128]{3,2,1,0:T(8,128)(2,1)}, bf16[128,4,8,128]{3,2,1,0:T(8,128)(2,1)S(1)}, u32[]{:S(2)}, u32[]{:S(2)}) collective-permute-start(bf16[128,4,8,128]{3,2,1,0:T(8,128)(2,1)} %bitcast.38), channel_id=1, source_target_pairs={{0,1},{1,0},{2,3},{3,2},{4,5},{5,4},{6,7},{7,6},{8,9},{9,8},{10,11... | collective-permute-start | bytes 3145736 | tf_op jit(solution)/shard_map/ppermute | solution.py:177
  7.4 3.3 %collective-permute-start.5 = (s32[1,8]{1,0:T(1,128)S(1)}, s32[1,8]{1,0:T(1,128)S(1)}, u32[]{:S(2)}, u32[]{:S(2)}) collective-permute-start(s32[1,8]{1,0:T(1,128)S(1)} %copy-done.2), channel_id=1, source_target_pairs={{0,1},{1,0},{2,3},{3,2},{4,5},{5,4},{6,7},{7,6},{8,9},{9,8},{10,11... | collective-permute-start | bytes 104 | tf_op jit(solution)/shard_map/ppermute | solution.py:179
  9.1 0.7 %copy-start.4 = (s32[4]{0:T(128)S(1)}, s32[4]{0:T(128)}, u32[]{:S(2)}) copy-start(s32[4]{0:T(128)} %constant.51.clone) | copy-start | bytes 52
  9.8 0.7 %copy-start.3 = (s32[128]{0:T(128)S(1)}, s32[128]{0:T(128)}, u32[]{:S(2)}) copy-start(s32[128]{0:T(128)} %param.8) | copy-start | bytes 1540
  10.6 1.2 %collective-permute-start.4 = (s32[128]{0:T(128)S(1)}, s32[128]{0:T(128)S(1)}, u32[]{:S(2)}, u32[]{:S(2)}) collective-permute-start(s32[128]{0:T(128)S(1)} %copy-done.3), channel_id=1, source_target_pairs={{0,1},{1,0},{2,3},{3,2},{4,5},{5,4},{6,7},{7,6},{8,9},{9,8},{10,11... | collective-permute-start | bytes 1544 | tf_op jit(solution)/shard_map/ppermute | solution.py:178
  12.3 4.6 %copy-start.1 = (s32[129]{0:T(256)S(1)}, s32[129]{0:T(256)}, u32[]{:S(2)}) copy-start(s32[129]{0:T(256)} %param.10) | copy-start | bytes 1552
  14.7 3.7 %collective-permute-start.6 = (f32[8,128]{1,0:T(8,128)S(1)}, f32[8,128]{1,0:T(8,128)S(1)}, u32[]{:S(2)}, u32[]{:S(2)}) collective-permute-start(f32[8,128]{1,0:T(8,128)S(1)} %shard_map.77), channel_id=1, source_target_pairs={{0,4},{4,0},{8,12},{12,8},{1,5},{5,1},{9,13},{13,9},{2,6},{6,2},{1... | collective-permute-start | bytes 12296 | tf_op jit(solution)/shard_map/ppermute | solution.py:189
  16.5 1.8 %collective-permute-start.7 = (f32[8,128]{1,0:T(8,128)S(1)}, f32[8,128]{1,0:T(8,128)S(1)}, u32[]{:S(2)}, u32[]{:S(2)}) collective-permute-start(f32[8,128]{1,0:T(8,128)S(1)} %shard_map.77), channel_id=1, source_target_pairs={{0,1},{1,0},{2,3},{3,2},{4,5},{5,4},{6,7},{7,6},{8,9},{9,8},{10,11... | collective-permute-start | bytes 12296 | tf_op jit(solution)/shard_map/ppermute | solution.py:190
  16.5 3.0 %collective-permute-start.8 = (f32[8,128]{1,0:T(8,128)S(1)}, f32[8,128]{1,0:T(8,128)S(1)}, u32[]{:S(2)}, u32[]{:S(2)}) collective-permute-start(f32[8,128]{1,0:T(8,128)S(1)} %shard_map.77), channel_id=1, source_target_pairs={{0,5},{1,4},{4,1},{5,0},{8,13},{9,12},{12,9},{13,8},{2,7},{3,6},{6... | collective-permute-start | bytes 12296 | tf_op jit(solution)/shard_map/ppermute | solution.py:191
  19.6 4.0 %collective-permute-start.9 = (f32[16,128]{1,0:T(8,128)S(1)}, f32[16,128]{1,0:T(8,128)S(1)}, u32[]{:S(2)}, u32[]{:S(2)}) collective-permute-start(f32[16,128]{1,0:T(8,128)S(1)} %pad_maximum_fusion.mine_ref), channel_id=1, source_target_pairs={{0,9},{1,8},{4,13},{5,12},{8,1},{9,0},{12,5},{13,4},{2,11},{3,10},... | collective-permute-start | bytes 24584 | tf_op jit(solution)/shard_map/ppermute | solution.py:200

commit v4 on v3

--- a/solution.py
+++ b/solution.py
@@ -175,8 +175,10 @@
     swap = xor_pairs(sub_count, 1)
     queries4 = queries.reshape(query_rows, groups_dev, per_group, head_dim)
     sibling_queries = lax.ppermute(queries4, "sub", swap)
-    positions = jnp.concatenate([obs_positions, lax.ppermute(obs_positions, "sub", swap)])
-    lists = jnp.concatenate([block_lists, lax.ppermute(block_lists, "sub", swap)])
+    facts = jnp.concatenate([obs_positions, block_lists.reshape(-1)])
+    both_facts = jnp.stack([facts, lax.ppermute(facts, "sub", swap)])
+    positions = both_facts[:, :query_rows].reshape(-1)
+    lists = both_facts[:, query_rows:]
     owners = jnp.bitwise_xor(ctx, jnp.array([0, *order], jnp.int32))
     bias = visible_bias(positions, lists, owners, local_keys)
 

time: 24.5 us -> 23.6 us (0.963)
  waiting for transfers between devices: 5.83 us -> 4.45 us
  starting transfers between devices: 10.2 us -> 11.4 us
  local copies, waits for them, and re-layouts: 2.4 us -> 1.72 us
    ppermute x3, waiting for transfers between devices: 0.01 us -> 1.43 us  [local(): lax.ppermute(own_keys, 'ctx', xor_pairs(ctx_count, distance))]
    ppermute x1, starting transfers between devices: 1.8 us -> 2.91 us  [local(): theirs = lax.ppermute(mine, ('ctx', 'sub'), pairs)]
    ppermute x2 -> x1, waiting for transfers between devices: 1.04 us -> 0.01 us  [local(): both_facts = jnp.stack([facts, lax.ppermute(facts, 'sub', swap)])]
    ppermute x1, starting transfers between devices: 1.86 us -> 0.82 us  [local(): near = lax.ppermute(mass, 'ctx', xor_pairs(ctx_count, 1))]
    ppermute x1, starting transfers between devices: 0.34 us -> 1.38 us  [local(): across = lax.ppermute(mass, ('ctx', 'sub'), xor_pairs(both_count, 3))]
    ppermute x1, waiting for transfers between devices: 1.22 us -> 0.18 us  [local(): across = lax.ppermute(mass, ('ctx', 'sub'), xor_pairs(both_count, 3))]
    ppermute x1, waiting for transfers between devices: 2.16 us -> 1.36 us  [local(): theirs = lax.ppermute(mine, ('ctx', 'sub'), pairs)]
    unnamed x12 -> x11, local copies, waits for them, and re-layouts: 2.24 us -> 1.58 us
  transfers between devices with their start and end apart: 10 -> 9, of which waited for: 4 -> 6; matrix products, arithmetic and copies ran while one was open for 8% -> 9% of each run, Pallas kernels for 0% -> 0%
where the time goes in v4:
time: 23.6 us; the launch traced here: 23.4 us
  starting transfers between devices  11.4 us (48%)
  waiting for transfers between devices  4.45 us (19%)
  Pallas kernels  3.12 us (13%)
  other arithmetic  1.96 us (8%)
  local copies, waits for them, and re-layouts  1.72 us (7%)
  between operations  0.74 us (3%)
    ppermute x3, starting transfers between devices, local(): lax.ppermute(own_keys, 'ctx', xor_pairs(ctx_count, distance))  5.71 us
    ppermute x1, starting transfers between devices, local(): theirs = lax.ppermute(mine, ('ctx', 'sub'), pairs)  2.91 us
    pallas_call x1, Pallas kernels, mass_call(): pl.pallas_call(kernel, out_shape=jax.ShapeDtypeStruct((groups * chunks, l...  2.36 us
    unnamed x11, local copies, waits for them, and re-layouts  1.58 us
    convert_element_type x2, other arithmetic, scaled_parts(): return [upper.astype(jnp.bfloat16), (scaled - upper).astype(jnp.bfloat16)]  1.45 us
    ppermute x3, waiting for transfers between devices, local(): lax.ppermute(own_keys, 'ctx', xor_pairs(ctx_count, distance))  1.43 us
    ppermute x1, waiting for transfers between devices, local(): near = lax.ppermute(mass, 'ctx', xor_pairs(ctx_count, 1))  1.39 us
    ppermute x1, starting transfers between devices, local(): across = lax.ppermute(mass, ('ctx', 'sub'), xor_pairs(both_count, 3))  1.38 us
  transfers between devices with their start and end apart: 9, of which 6 were waited for; matrix products, arithmetic and copies ran while one was open for 9% of the time, Pallas kernels for 0%

profile of v4, /device:TPU:0, one launch (start us, length us, event | category | flops | bytes accessed | tf_op | source)
XLA Modules:
  0.0 23.4 jit_solution(5706665634798879260)
XLA Ops:
  0.7 0.9 %copy-done = bf16[128,4,128]{2,1,0:T(4,128)(2,1)S(1)} copy-done((bf16[128,4,128]{2,1,0:T(4,128)(2,1)S(1)}, bf16[128,4,128]{2,1,0:T(4,128)(2,1)}, u32[]{:S(2)}) %copy-start) | copy-done | bytes 131096
  1.5 0.1 constant_dynamic-slice_fusion
  1.7 4.1 %collective-permute-start.1 = (bf16[2,128,128]{2,1,0:T(8,128)(2,1)S(1)}, bf16[2,128,128]{2,1,0:T(8,128)(2,1)S(1)}, u32[]{:S(2)}, u32[]{:S(2)}) collective-permute-start(bf16[2,128,128]{2,1,0:T(8,128)(2,1)S(1)} %bitcast.40), channel_id=1, source_target_pairs={{0,8},{4,12},{8,0},{12,4},{1,9},{5,13},{9,1},{13,5},{2,10},{6,14},... | collective-permute-start | bytes 196616 | tf_op jit(solution)/shard_map/ppermute | solution.py:171
  5.8 1.3 %collective-permute-start.2 = (bf16[2,128,128]{2,1,0:T(8,128)(2,1)S(1)}, bf16[2,128,128]{2,1,0:T(8,128)(2,1)S(1)}, u32[]{:S(2)}, u32[]{:S(2)}) collective-permute-start(bf16[2,128,128]{2,1,0:T(8,128)(2,1)S(1)} %bitcast.41), channel_id=1, source_target_pairs={{0,12},{4,8},{8,4},{12,0},{1,13},{5,9},{9,5},{13,1},{2,14},{6,10},... | collective-permute-start | bytes 196616 | tf_op jit(solution)/shard_map/ppermute | solution.py:171
  7.1 0.2 collective-permute-start.3
  7.5 0.5 %collective-permute-start = (bf16[128,4,8,128]{3,2,1,0:T(8,128)(2,1)}, bf16[128,4,8,128]{3,2,1,0:T(8,128)(2,1)S(1)}, u32[]{:S(2)}, u32[]{:S(2)}) collective-permute-start(bf16[128,4,8,128]{3,2,1,0:T(8,128)(2,1)} %bitcast.44), channel_id=1, source_target_pairs={{0,1},{1,0},{2,3},{3,2},{4,5},{5,4},{6,7},{7,6},{8,9},{9,8},{10,11... | collective-permute-start | bytes 3145736 | tf_op jit(solution)/shard_map/ppermute | solution.py:177
  8.0 0.7 %copy-done.4 = s32[4]{0:T(128)S(1)} copy-done((s32[4]{0:T(128)S(1)}, s32[4]{0:T(128)}, u32[]{:S(2)}) %copy-start.4) | copy-done | bytes 40
  8.6 0.1 add_select_fusion
  8.8 1.2 %fusion = (bf16[128,2,8,128]{3,2,1,0:T(8,128)(2,1)S(1)}, bf16[128,2,8,128]{3,2,1,0:T(8,128)(2,1)S(1)}) fusion(bf16[128,4,8,128]{3,2,1,0:T(8,128)(2,1)} %bitcast.45, s32[]{:T(128)S(6)} %select_n.31), kind=kLoop, calls=%fused_computation.4 | loop fusion | flops 1572864 | bytes 1572868 | tf_op jit(solution)/shard_map/convert_element_type | solution.py:37
  10.1 0.1 compare_reduce_fusion
  10.2 0.2 fusion.3.refs_8_
  10.4 0.1 collective-permute-done
  10.5 0.2 fusion.1
  10.7 1.3 %collective-permute-done.2.refs_6_ = bf16[2,128,128]{2,1,0:T(8,128)(2,1)S(1)} collective-permute-done((bf16[2,128,128]{2,1,0:T(8,128)(2,1)S(1)}, bf16[2,128,128]{2,1,0:T(8,128)(2,1)S(1)}, u32[]{:S(2)}, u32[]{:S(2)}) %collective-permute-start.2) | collective-permute-done | bytes 65568 | tf_op jit(solution)/shard_map/ppermute | solution.py:171
  12.0 0.1 collective-permute-done.3.refs_7_
  12.1 2.4 %shard_map.77 = f32[8,128]{1,0:T(8,128)S(1)} custom-call(bf16[128,2,8,128]{3,2,1,0:T(8,128)(2,1)S(1)} %get-tuple-element.7.refs_0_, bf16[128,2,8,128]{3,2,1,0:T(8,128)(2,1)S(1)} %get-tuple-element.6.refs_1_, bf16[128,2,8,128]{3,2,1,0:T(8,128)(2,1)S(1)} %get-tuple-element.5.refs_2_, bf16[128,2,8,128]{3,2,1,0:T(8,128)(2,1)S(1)} %get-tuple-element.4.refs_3_, ...), custom_call_target="tpu_custom_call" | custom-call | flops 536870912 | bytes 1048576 | tf_op jit(solution)/shard_map/pallas_call | solution.py:94
  14.5 0.8 %collective-permute-start.5 = (f32[8,128]{1,0:T(8,128)S(1)}, f32[8,128]{1,0:T(8,128)S(1)}, u32[]{:S(2)}, u32[]{:S(2)}) collective-permute-start(f32[8,128]{1,0:T(8,128)S(1)} %shard_map.77), channel_id=1, source_target_pairs={{0,4},{4,0},{8,12},{12,8},{1,5},{5,1},{9,13},{13,9},{2,6},{6,2},{1... | collective-permute-start | bytes 12296 | tf_op jit(solution)/shard_map/ppermute | solution.py:191
  15.3 1.4 %collective-permute-start.7 = (f32[8,128]{1,0:T(8,128)S(1)}, f32[8,128]{1,0:T(8,128)S(1)}, u32[]{:S(2)}, u32[]{:S(2)}) collective-permute-start(f32[8,128]{1,0:T(8,128)S(1)} %shard_map.77), channel_id=1, source_target_pairs={{0,5},{1,4},{4,1},{5,0},{8,13},{9,12},{12,9},{13,8},{2,7},{3,6},{6... | collective-permute-start | bytes 12296 | tf_op jit(solution)/shard_map/ppermute | solution.py:193
  16.7 0.1 slice_bitcast_fusion.1
  16.8 1.4 %collective-permute-done.5 = f32[8,128]{1,0:T(8,128)S(1)} collective-permute-done((f32[8,128]{1,0:T(8,128)S(1)}, f32[8,128]{1,0:T(8,128)S(1)}, u32[]{:S(2)}, u32[]{:S(2)}) %collective-permute-start.5) | collective-permute-done | bytes 4128 | tf_op jit(solution)/shard_map/ppermute | solution.py:191
  18.2 0.2 collective-permute-done.7
  18.3 2.9 %collective-permute-start.8 = (f32[16,128]{1,0:T(8,128)S(1)}, f32[16,128]{1,0:T(8,128)S(1)}, u32[]{:S(2)}, u32[]{:S(2)}) collective-permute-start(f32[16,128]{1,0:T(8,128)S(1)} %pad_maximum_fusion.mine_ref), channel_id=1, source_target_pairs={{0,9},{1,8},{4,13},{5,12},{8,1},{9,0},{12,5},{13,4},{2,11},{3,10},... | collective-permute-start | bytes 24584 | tf_op jit(solution)/shard_map/ppermute | solution.py:202
  21.3 1.4 %collective-permute-done.8.theirs_ref = f32[16,128]{1,0:T(8,128)S(1)} collective-permute-done((f32[16,128]{1,0:T(8,128)S(1)}, f32[16,128]{1,0:T(8,128)S(1)}, u32[]{:S(2)}, u32[]{:S(2)}) %collective-permute-start.8) | collective-permute-done | bytes 8224 | tf_op jit(solution)/shard_map/ppermute | solution.py:202
  22.6 0.8 %shard_map.78 = (f32[4,128]{1,0:T(4,128)}, f32[4,128]{1,0:T(4,128)}) custom-call(f32[16,128]{1,0:T(8,128)S(1)} %pad_maximum_fusion.mine_ref, f32[16,128]{1,0:T(8,128)S(1)} %collective-permute-done.8.theirs_ref, s32[2,128]{1,0:T(2,128)S(1)} %pad_add_fusion.2.edges_ref), custom_call_target="tpu_custom_call" | custom-call | tf_op jit(solution)/shard_map/pallas_call | solution.py:141
  (23 shorter events, 0.2 us)
Async XLA Ops:
  0.6 0.9 %copy-start = (bf16[128,4,128]{2,1,0:T(4,128)(2,1)S(1)}, bf16[128,4,128]{2,1,0:T(4,128)(2,1)}, u32[]{:S(2)}) copy-start(bf16[128,4,128]{2,1,0:T(4,128)(2,1)} %param.7) | copy-start | bytes 393220
  1.6 5.7 %copy-start.2 = (s32[1,8]{1,0:T(1,128)S(1)}, s32[1,8]{1,0:T(1,128)}, u32[]{:S(2)}) copy-start(s32[1,8]{1,0:T(1,128)} %param.9) | copy-start | bytes 100
  1.6 5.7 %copy-start.3 = (s32[128]{0:T(128)S(1)}, s32[128]{0:T(128)}, u32[]{:S(2)}) copy-start(s32[128]{0:T(128)} %param.8) | copy-start | bytes 1540
  1.7 9.0 %collective-permute-start.1 = (bf16[2,128,128]{2,1,0:T(8,128)(2,1)S(1)}, bf16[2,128,128]{2,1,0:T(8,128)(2,1)S(1)}, u32[]{:S(2)}, u32[]{:S(2)}) collective-permute-start(bf16[2,128,128]{2,1,0:T(8,128)(2,1)S(1)} %bitcast.40), channel_id=1, source_target_pairs={{0,8},{4,12},{8,0},{12,4},{1,9},{5,13},{9,1},{13,5},{2,10},{6,14},... | collective-permute-start | bytes 196616 | tf_op jit(solution)/shard_map/ppermute | solution.py:171
  5.8 6.2 %collective-permute-start.2 = (bf16[2,128,128]{2,1,0:T(8,128)(2,1)S(1)}, bf16[2,128,128]{2,1,0:T(8,128)(2,1)S(1)}, u32[]{:S(2)}, u32[]{:S(2)}) collective-permute-start(bf16[2,128,128]{2,1,0:T(8,128)(2,1)S(1)} %bitcast.41), channel_id=1, source_target_pairs={{0,12},{4,8},{8,4},{12,0},{1,13},{5,9},{9,5},{13,1},{2,14},{6,10},... | collective-permute-start | bytes 196616 | tf_op jit(solution)/shard_map/ppermute | solution.py:171
  7.1 5.0 %collective-permute-start.3 = (bf16[2,128,128]{2,1,0:T(8,128)(2,1)S(1)}, bf16[2,128,128]{2,1,0:T(8,128)(2,1)S(1)}, u32[]{:S(2)}, u32[]{:S(2)}) collective-permute-start(bf16[2,128,128]{2,1,0:T(8,128)(2,1)S(1)} %bitcast.42), channel_id=1, source_target_pairs={{0,4},{4,0},{8,12},{12,8},{1,5},{5,1},{9,13},{13,9},{2,6},{6,2},{1... | collective-permute-start | bytes 196616 | tf_op jit(solution)/shard_map/ppermute | solution.py:171
  7.4 2.6 %collective-permute-start.4 = (s32[136]{0:T(256)S(1)}, s32[136]{0:T(256)S(1)}, u32[]{:S(2)}, u32[]{:S(2)}) collective-permute-start(s32[136]{0:T(256)S(1)} %pad_add_fusion.1), channel_id=1, source_target_pairs={{0,1},{1,0},{2,3},{3,2},{4,5},{5,4},{6,7},{7,6},{8,9},{9,8},{10,11... | collective-permute-start | bytes 1640 | tf_op jit(solution)/shard_map/ppermute | solution.py:179
  7.5 3.0 %collective-permute-start = (bf16[128,4,8,128]{3,2,1,0:T(8,128)(2,1)}, bf16[128,4,8,128]{3,2,1,0:T(8,128)(2,1)S(1)}, u32[]{:S(2)}, u32[]{:S(2)}) collective-permute-start(bf16[128,4,8,128]{3,2,1,0:T(8,128)(2,1)} %bitcast.44), channel_id=1, source_target_pairs={{0,1},{1,0},{2,3},{3,2},{4,5},{5,4},{6,7},{7,6},{8,9},{9,8},{10,11... | collective-permute-start | bytes 3145736 | tf_op jit(solution)/shard_map/ppermute | solution.py:177
  8.0 0.7 %copy-start.4 = (s32[4]{0:T(128)S(1)}, s32[4]{0:T(128)}, u32[]{:S(2)}) copy-start(s32[4]{0:T(128)} %constant.51.clone) | copy-start | bytes 52
  12.1 4.6 %copy-start.1 = (s32[129]{0:T(256)S(1)}, s32[129]{0:T(256)}, u32[]{:S(2)}) copy-start(s32[129]{0:T(256)} %param.10) | copy-start | bytes 1552
  14.5 3.7 %collective-permute-start.5 = (f32[8,128]{1,0:T(8,128)S(1)}, f32[8,128]{1,0:T(8,128)S(1)}, u32[]{:S(2)}, u32[]{:S(2)}) collective-permute-start(f32[8,128]{1,0:T(8,128)S(1)} %shard_map.77), channel_id=1, source_target_pairs={{0,4},{4,0},{8,12},{12,8},{1,5},{5,1},{9,13},{13,9},{2,6},{6,2},{1... | collective-permute-start | bytes 12296 | tf_op jit(solution)/shard_map/ppermute | solution.py:191
  15.3 2.9 %collective-permute-start.6 = (f32[8,128]{1,0:T(8,128)S(1)}, f32[8,128]{1,0:T(8,128)S(1)}, u32[]{:S(2)}, u32[]{:S(2)}) collective-permute-start(f32[8,128]{1,0:T(8,128)S(1)} %shard_map.77), channel_id=1, source_target_pairs={{0,1},{1,0},{2,3},{3,2},{4,5},{5,4},{6,7},{7,6},{8,9},{9,8},{10,11... | collective-permute-start | bytes 12296 | tf_op jit(solution)/shard_map/ppermute | solution.py:192
  15.3 3.0 %collective-permute-start.7 = (f32[8,128]{1,0:T(8,128)S(1)}, f32[8,128]{1,0:T(8,128)S(1)}, u32[]{:S(2)}, u32[]{:S(2)}) collective-permute-start(f32[8,128]{1,0:T(8,128)S(1)} %shard_map.77), channel_id=1, source_target_pairs={{0,5},{1,4},{4,1},{5,0},{8,13},{9,12},{12,9},{13,8},{2,7},{3,6},{6... | collective-permute-start | bytes 12296 | tf_op jit(solution)/shard_map/ppermute | solution.py:193
  18.3 4.3 %collective-permute-start.8 = (f32[16,128]{1,0:T(8,128)S(1)}, f32[16,128]{1,0:T(8,128)S(1)}, u32[]{:S(2)}, u32[]{:S(2)}) collective-permute-start(f32[16,128]{1,0:T(8,128)S(1)} %pad_maximum_fusion.mine_ref), channel_id=1, source_target_pairs={{0,9},{1,8},{4,13},{5,12},{8,1},{9,0},{12,5},{13,4},{2,11},{3,10},... | collective-permute-start | bytes 24584 | tf_op jit(solution)/shard_map/ppermute | solution.py:202
